TPU v7x, 32 devices: a whole 2x2x4 slice. The times are simulated.
32 devices in a mesh: dp: 4 (over x, core), gx: 2 (over y), gy: 4 (over z).
Axes of the slice: x: 2, y: 2, z: 4, core: 2. Of those that a mesh axis runs over, the one named last changes fastest.
Arguments:
- inputs: bfloat16 [4096, 960], P(('dp', 'gx', 'gy')), may hold values from -6 to 6
- segments: int32 [4096], P('dp'), may hold values from 0 to 15, never falling along the last dimension, each value on 1 to 512 neighbouring positions
- attn_gain: float32 [960], replicated, may hold values from 0.5 to 1.5
- query_weight: bfloat16 [960, 960], P('gx', 'gy'), may hold values from -1.6 to 1.6
- key_weight: bfloat16 [960, 320], P('gx', 'gy'), may hold values from -1.6 to 1.6
- value_weight: bfloat16 [960, 320], P('gx', 'gy'), may hold values from -0.1875 to 0.1875
- output_weight: bfloat16 [960, 960], P('gx', 'gy'), may hold values from -0.75 to 0.75
- mlp_gain: float32 [960], replicated, may hold values from 0.5 to 1.5
- gate_weight: bfloat16 [960, 2560], P('gx', 'gy'), may hold values from -0.1875 to 0.1875
- up_weight: bfloat16 [960, 2560], P('gx', 'gy'), may hold values from -0.1875 to 0.1875
- down_weight: bfloat16 [2560, 960], P('gx', 'gy'), may hold values from -0.125 to 0.125
- cotangent: bfloat16 [4096, 960], P(('dp', 'gx', 'gy')), may hold values from -6 to 6
Outputs:
- layer_out: bfloat16 [4096, 960], P(('dp', 'gx', 'gy'))
- input_grad: bfloat16 [4096, 960], P(('dp', 'gx', 'gy'))
- query_grad: float32 [960, 960], P('gx', 'gy')
- key_grad: float32 [960, 320], P('gx', 'gy')
- value_grad: float32 [960, 320], P('gx', 'gy')
- output_grad: float32 [960, 960], P('gx', 'gy')
- gate_grad: float32 [960, 2560], P('gx', 'gy')
- up_grad: float32 [960, 2560], P('gx', 'gy')
- down_grad: float32 [2560, 960], P('gx', 'gy')
- attgain_grad: float32 [960], replicated
- mlpgain_grad: float32 [960], replicated
Inputs may be any that keep to these rules, and one draw needn't show every extreme that they name: `segments`: segment numbers never fall along the tokens; a document may run on past the end of a sequence.
All inputs are finite; a program needn't handle non-finite values.
Results may differ from a plain program's by a relative error of at most 0.04.
Values may be sent and summed in bfloat16 or wider, within the bound.
A program may use at most 128 MiB of HBM per device.

v0:
```python
import jax
import jax.numpy as jnp
from jax import lax
from jax.sharding import PartitionSpec as P

QUERY_HEADS = 15
KEY_VALUE_HEADS = 5
HEAD_WIDTH = 64
SEQUENCE_LENGTH = 1024


THETA = 100000.0
EPSILON = 1e-05
MASKED = -1e30


def rope_angles(positions):
    half_dim = HEAD_WIDTH // 2
    inverse = THETA ** (-(jnp.arange(half_dim, dtype=jnp.float32) * 2.0 / HEAD_WIDTH))
    angles = positions[:, None] * inverse[None, :]
    return (jnp.cos(angles)[:, None, :], jnp.sin(angles)[:, None, :])


def rotate(values, cos_table, sin_table):
    item_count = values.shape[0]
    shaped = values.reshape(item_count, -1, HEAD_WIDTH)
    half_dim = HEAD_WIDTH // 2
    front_part = shaped[:, :, :half_dim]
    back_part = shaped[:, :, half_dim:]
    turned = jnp.concatenate(
        [
            front_part * cos_table - back_part * sin_table,
            back_part * cos_table + front_part * sin_table,
        ],
        axis=2,
    )
    return turned.reshape(item_count, -1)


def unrotate(values, cos_table, sin_table):
    item_count = values.shape[0]
    shaped = values.reshape(item_count, -1, HEAD_WIDTH)
    half_dim = HEAD_WIDTH // 2
    front_part = shaped[:, :, :half_dim]
    back_part = shaped[:, :, half_dim:]
    turned = jnp.concatenate(
        [
            front_part * cos_table + back_part * sin_table,
            back_part * cos_table - front_part * sin_table,
        ],
        axis=2,
    )
    return turned.reshape(item_count, -1)


def normalize(values, gain):
    rms_rows = lax.rsqrt(jnp.mean(values * values, axis=1, keepdims=True) + EPSILON)
    unit_rows = values * rms_rows
    return (rms_rows, unit_rows, (unit_rows * gain).astype(jnp.bfloat16))


def normalize_back(dnormed, gain, rms_rows, unit_rows):
    scaled = dnormed * gain
    dvalues = rms_rows * (scaled - unit_rows * jnp.mean(scaled * unit_rows, axis=1, keepdims=True))
    return (dvalues, jnp.sum(dnormed * unit_rows, axis=0))


def weight_product(left, right):
    return lax.dot_general(
        left, right, (((0,), (0,)), ((), ())), preferred_element_type=jnp.float32
    )


def back_product(left, right):
    return lax.dot_general(
        left, right, (((1,), (1,)), ((), ())), preferred_element_type=jnp.float32
    )


def pack_columns(parts):
    fanout = lax.axis_size("gy")
    count_of_rows = parts[0].shape[0]
    blocks = [column_part.reshape(count_of_rows, fanout, -1) for column_part in parts]
    return jnp.concatenate(blocks, axis=2).reshape(count_of_rows, -1)


def unpack_columns(packed, widths):
    fanout = lax.axis_size("gy")
    count_of_rows = packed.shape[0]
    shaped = packed.reshape(count_of_rows, fanout, -1)
    outputs = []
    offset = 0
    for block_width in widths:
        outputs.append(shaped[:, :, offset : offset + block_width].reshape(count_of_rows, -1))
        offset = offset + block_width
    return outputs


def spread(local_rows):
    stacked = lax.all_gather(local_rows, "gy", axis=0, tiled=True)
    return lax.all_to_all(stacked, "gx", split_axis=1, concat_axis=0, tiled=True)


def collect(spread_inputs, weight, widths):
    summed = lax.psum_scatter(
        jnp.dot(spread_inputs, weight, preferred_element_type=jnp.float32).astype(jnp.bfloat16),
        "gx",
        scatter_dimension=0,
        tiled=True,
    )
    moved = lax.all_to_all(summed, "gy", split_axis=0, concat_axis=1, tiled=True)
    return unpack_columns(moved, widths)


def spread_grads(parts):
    moved = lax.all_to_all(pack_columns(parts), "gy", split_axis=1, concat_axis=0, tiled=True)
    return lax.all_gather(moved, "gx", axis=0, tiled=True)


def gather_inputs(full_grads, weight):
    fanin = lax.axis_size("gx")
    fanout = lax.axis_size("gy")
    count_of_rows = full_grads.shape[0] // (fanin * fanout)
    reordered = (
        full_grads.reshape(fanin, fanout, count_of_rows, -1)
        .transpose(1, 0, 2, 3)
        .reshape(fanin * fanout * count_of_rows, -1)
    )
    summed = lax.psum_scatter(
        back_product(reordered, weight).astype(jnp.bfloat16), "gy", scatter_dimension=0, tiled=True
    ).astype(jnp.float32)
    return lax.all_to_all(
        summed.astype(jnp.bfloat16), "gx", split_axis=0, concat_axis=1, tiled=True
    ).astype(summed.dtype)


def head_views(rotated_query, key_sequence, value_sequence):
    query_groups = QUERY_HEADS // KEY_VALUE_HEADS
    query_head_split = rotated_query.reshape(
        rotated_query.shape[0], KEY_VALUE_HEADS, query_groups, HEAD_WIDTH
    )
    key_head_split = key_sequence.reshape(key_sequence.shape[0], KEY_VALUE_HEADS, HEAD_WIDTH)
    value_head_split = value_sequence.reshape(value_sequence.shape[0], KEY_VALUE_HEADS, HEAD_WIDTH)
    return (query_head_split, key_head_split, value_head_split)


def masked_scores(query_head_split, key_head_split, allowed):
    scores = jnp.einsum(
        "tkgd,ukd->kgtu", query_head_split, key_head_split, preferred_element_type=jnp.float32
    ) * HEAD_WIDTH ** (-0.5)
    return jnp.where(allowed, scores, MASKED)


def attend(rotated_query, key_sequence, value_sequence, allowed):
    query_head_split, key_head_split, value_head_split = head_views(
        rotated_query, key_sequence, value_sequence
    )
    scores = masked_scores(query_head_split, key_head_split, allowed)
    highest = jnp.max(scores, axis=3, keepdims=True)
    logsum = highest + jnp.log(jnp.sum(jnp.exp(scores - highest), axis=3, keepdims=True))
    probs = jnp.exp(scores - logsum).astype(jnp.bfloat16)
    attention_mixture = jnp.einsum(
        "kgtu,ukd->tkgd", probs, value_head_split, preferred_element_type=jnp.float32
    )
    return (attention_mixture.reshape(rotated_query.shape[0], -1).astype(jnp.bfloat16), logsum)


def attend_back(
    rotated_query,
    key_sequence,
    value_sequence,
    allowed,
    logsum,
    attention_mixture,
    mixture_gradient,
):
    query_head_split, key_head_split, value_head_split = head_views(
        rotated_query, key_sequence, value_sequence
    )
    count_of_rows = rotated_query.shape[0]
    query_groups = QUERY_HEADS // KEY_VALUE_HEADS
    soft_weights = jnp.exp(masked_scores(query_head_split, key_head_split, allowed) - logsum)
    probs = soft_weights.astype(jnp.bfloat16)
    mixture_head_gradient = mixture_gradient.reshape(
        count_of_rows, KEY_VALUE_HEADS, query_groups, HEAD_WIDTH
    )
    mixture_heads = attention_mixture.reshape(
        count_of_rows, KEY_VALUE_HEADS, query_groups, HEAD_WIDTH
    )
    row_delta = jnp.sum(
        mixture_heads.astype(jnp.float32) * mixture_head_gradient.astype(jnp.float32), axis=3
    )
    row_delta = jnp.transpose(row_delta, (1, 2, 0))[:, :, :, None]
    dprobs = jnp.einsum(
        "tkgd,ukd->kgtu",
        mixture_head_gradient,
        value_head_split,
        preferred_element_type=jnp.float32,
    )
    dscores = (soft_weights * (dprobs - row_delta)).astype(jnp.bfloat16)
    dquery = jnp.einsum(
        "kgtu,ukd->tkgd", dscores, key_head_split, preferred_element_type=jnp.float32
    ).reshape(count_of_rows, -1) * HEAD_WIDTH ** (-0.5)
    dkeys = jnp.einsum(
        "kgtu,tkgd->ukd", dscores, query_head_split, preferred_element_type=jnp.float32
    ).reshape(key_sequence.shape[0], -1) * HEAD_WIDTH ** (-0.5)
    dvalues = jnp.einsum(
        "kgtu,tkgd->ukd", probs, mixture_head_gradient, preferred_element_type=jnp.float32
    ).reshape(key_sequence.shape[0], -1)
    return (dquery, dkeys, dvalues)


def on_device(
    inputs,
    segments,
    attn_gain,
    query_weight,
    key_weight,
    value_weight,
    output_weight,
    mlp_gain,
    gate_weight,
    up_weight,
    down_weight,
    cotangent,
):
    count_of_rows = inputs.shape[0]
    fanout = lax.axis_size("gy")
    begin_row = (lax.axis_index("gx") * fanout + lax.axis_index("gy")) * count_of_rows
    seq_begin = begin_row // SEQUENCE_LENGTH * SEQUENCE_LENGTH
    local_places = begin_row - seq_begin + jnp.arange(count_of_rows)
    cos_table, sin_table = rope_angles(local_places.astype(jnp.float32))
    query_segs = lax.dynamic_slice_in_dim(segments, begin_row, count_of_rows, 0)
    allowed = (jnp.arange(SEQUENCE_LENGTH)[None, :] <= local_places[:, None]) & (
        query_segs[:, None] == segments[None, :]
    )
    residual = inputs.astype(jnp.float32)
    rms_one, unit_one, normed_one = normalize(residual, attn_gain)
    spread_one = spread(normed_one)
    attn_weight = jnp.concatenate([query_weight, key_weight, value_weight], axis=1)
    attn_widths = [query_weight.shape[1], key_weight.shape[1], value_weight.shape[1]]
    query_rows, key_rows, value_row_list = collect(spread_one, attn_weight, attn_widths)
    rotated_query = rotate(query_rows.astype(jnp.float32), cos_table, sin_table).astype(
        jnp.bfloat16
    )
    rotated_key = rotate(key_rows.astype(jnp.float32), cos_table, sin_table).astype(jnp.bfloat16)
    key_all, value_all = (
        lax.all_gather(rotated_key, ("gx", "gy"), axis=0, tiled=True),
        lax.all_gather(value_row_list, ("gx", "gy"), axis=0, tiled=True),
    )
    attention_mixture, logsum = attend(rotated_query, key_all, value_all, allowed)
    mixed_spread = spread(attention_mixture)
    attn_out = collect(mixed_spread, output_weight, [output_weight.shape[1]])[0]
    hidden = residual + attn_out.astype(jnp.float32)
    rms_two, unit_two, normed_two = normalize(hidden, mlp_gain)
    spread_two = spread(normed_two)
    mlp_weight = jnp.concatenate([gate_weight, up_weight], axis=1)
    gate_width = gate_weight.shape[1]
    gate_rows, up_rows = collect(spread_two, mlp_weight, [gate_width, up_weight.shape[1]])
    gate_float = gate_rows.astype(jnp.float32)
    up_float = up_rows.astype(jnp.float32)
    sigmoid_gate = jax.nn.sigmoid(gate_float)
    activated = (gate_float * sigmoid_gate * up_float).astype(jnp.bfloat16)
    act_spread = spread(activated)
    mlp_out = collect(act_spread, down_weight, [down_weight.shape[1]])[0]
    layer_out = (hidden + mlp_out.astype(jnp.float32)).astype(jnp.bfloat16)
    cot_spread = spread_grads([cotangent])
    down_grad = weight_product(act_spread, cot_spread)
    dactivated = gather_inputs(cot_spread, down_weight)
    gate_delta = (
        dactivated * up_float * sigmoid_gate * (1.0 + gate_float * (1.0 - sigmoid_gate))
    ).astype(jnp.bfloat16)
    up_delta = (dactivated * gate_float * sigmoid_gate).astype(jnp.bfloat16)
    mlp_spread_grads = spread_grads([gate_delta, up_delta])
    mlp_grads = weight_product(spread_two, mlp_spread_grads)
    gate_grad = mlp_grads[:, :gate_width]
    up_grad = mlp_grads[:, gate_width:]
    dnormed_two = gather_inputs(mlp_spread_grads, mlp_weight)
    dhidden_norm, mlpgain_part = normalize_back(dnormed_two, mlp_gain, rms_two, unit_two)
    dhidden = cotangent.astype(jnp.float32) + dhidden_norm
    dhidden_bf = dhidden.astype(jnp.bfloat16)
    hidden_spread = spread_grads([dhidden_bf])
    output_grad = weight_product(mixed_spread, hidden_spread)
    mixture_gradient = gather_inputs(hidden_spread, output_weight).astype(jnp.bfloat16)
    dquery_rot, dkey_seq, dvalue_seq = attend_back(
        rotated_query, key_all, value_all, allowed, logsum, attention_mixture, mixture_gradient
    )
    dkey_rot, dvalue_rows = (
        lax.psum_scatter(
            dkey_seq.astype(jnp.bfloat16), ("gx", "gy"), scatter_dimension=0, tiled=True
        ).astype(jnp.float32),
        lax.psum_scatter(
            dvalue_seq.astype(jnp.bfloat16), ("gx", "gy"), scatter_dimension=0, tiled=True
        ).astype(jnp.float32),
    )
    dquery = unrotate(dquery_rot, cos_table, sin_table).astype(jnp.bfloat16)
    dkey = unrotate(dkey_rot, cos_table, sin_table).astype(jnp.bfloat16)
    dvalue_bf = dvalue_rows.astype(jnp.bfloat16)
    attn_spread_grads = spread_grads([dquery, dkey, dvalue_bf])
    attn_grads = weight_product(spread_one, attn_spread_grads)
    query_grad = attn_grads[:, : attn_widths[0]]
    key_grad = attn_grads[:, attn_widths[0] : attn_widths[0] + attn_widths[1]]
    value_grad = attn_grads[:, attn_widths[0] + attn_widths[1] :]
    dnormed_one = gather_inputs(attn_spread_grads, attn_weight)
    dresidual, attgain_part = normalize_back(dnormed_one, attn_gain, rms_one, unit_one)
    input_grad = (dhidden + dresidual).astype(jnp.bfloat16)
    attgain_grad, mlpgain_grad = lax.psum((attgain_part, mlpgain_part), ("dp", "gx", "gy"))
    query_grad, key_grad, value_grad, output_grad, gate_grad, up_grad, down_grad = (
        lax.psum(query_grad.astype(jnp.bfloat16), "dp").astype(jnp.float32),
        lax.psum(key_grad.astype(jnp.bfloat16), "dp").astype(jnp.float32),
        lax.psum(value_grad.astype(jnp.bfloat16), "dp").astype(jnp.float32),
        lax.psum(output_grad.astype(jnp.bfloat16), "dp").astype(jnp.float32),
        lax.psum(gate_grad.astype(jnp.bfloat16), "dp").astype(jnp.float32),
        lax.psum(up_grad.astype(jnp.bfloat16), "dp").astype(jnp.float32),
        lax.psum(down_grad.astype(jnp.bfloat16), "dp").astype(jnp.float32),
    )
    return (
        layer_out,
        input_grad,
        query_grad,
        key_grad,
        value_grad,
        output_grad,
        gate_grad,
        up_grad,
        down_grad,
        attgain_grad,
        mlpgain_grad,
    )


def solution(mesh):
    return jax.shard_map(
        on_device,
        mesh=mesh,
        in_specs=(
            P(("dp", "gx", "gy"), None),
            P("dp"),
            P(),
            P("gx", "gy"),
            P("gx", "gy"),
            P("gx", "gy"),
            P("gx", "gy"),
            P(),
            P("gx", "gy"),
            P("gx", "gy"),
            P("gx", "gy"),
            P(("dp", "gx", "gy"), None),
        ),
        out_specs=(
            P(("dp", "gx", "gy"), None),
            P(("dp", "gx", "gy"), None),
            P("gx", "gy"),
            P("gx", "gy"),
            P("gx", "gy"),
            P("gx", "gy"),
            P("gx", "gy"),
            P("gx", "gy"),
            P("gx", "gy"),
            P(),
            P(),
        ),
        check_vma=False,
    )
```

profile of v0, /device:TPU:0, one launch (start us, length us, event | category | flops | bytes accessed | tf_op | source)
XLA Modules:
  0.0 930.8 jit_solution(6093899341836011668)
XLA Ops:
  9.5 23.1 %all_gather.30 = bf16[512,960]{0,1:T(8,128)(2,1)} all-gather(bf16[128,960]{0,1:T(8,128)(2,1)S(1)} %fusion.24), channel_id=1, replica_groups=mesh['dp'=4,'gx'=2,'gy'=4] {'gy'}, dimensions={0}, use_global_device_ids=true | all-gather | bytes 1228800 | tf_op jit(solution)/shard_map/all_gather | solution.py:100
  32.6 3.6 all-to-all-start
  36.6 11.5 %all-to-all-done = bf16[512,2,480]{0,2,1:T(8,128)(2,1)S(1)} async-done(((bf16[512,2,480]{0,2,1:T(8,128)(2,1)}), bf16[512,2,480]{0,2,1:T(8,128)(2,1)S(1)}, u32[]{:S(2)}, u32[]{:S(2)}) %all-to-all-start) | async-done | bytes 983072 | tf_op jit(solution)/shard_map/all_to_all | solution.py:101
  50.9 17.1 %reduce-scatter.15.cloned.1.call-done = bf16[512,400]{0,1:T(8,128)(2,1)} async-done(((bf16[1024,400]{0,1:T(8,128)(2,1)}), bf16[512,400]{0,1:T(8,128)(2,1)}) %reduce-scatter.15.cloned.1.call-update) | async-done | bytes 409616 | tf_op jit(solution)/shard_map/reduce_scatter | solution.py:105
  69.8 4.6 all-to-all-start.1
  74.9 11.4 %all-to-all-done.1 = bf16[4,128,400]{1,2,0:T(8,128)(2,1)S(1)} async-done(((bf16[4,128,400]{1,2,0:T(8,128)(2,1)}), bf16[4,128,400]{1,2,0:T(8,128)(2,1)S(1)}, u32[]{:S(2)}, u32[]{:S(2)}) %all-to-all-start.1) | async-done | bytes 409632 | tf_op jit(solution)/shard_map/all_to_all | solution.py:111
  86.6 29.0 %all_gather.32 = bf16[1024,320]{0,1:T(8,128)(2,1)S(1)} all-gather(bf16[128,320]{0,1:T(8,128)(2,1)S(1)} %bitcast.306), channel_id=1, replica_groups=mesh['dp'=4,'gx'=2,'gy'=4] {'gx','gy'}, dimensions={0}, use_global_device_ids=true | all-gather | bytes 737280 | tf_op jit(solution)/shard_map/all_gather | solution.py:248
  118.6 30.4 %all_gather.31 = bf16[1024,320]{0,1:T(8,128)(2,1)S(1)} all-gather(bf16[128,320]{0,1:T(8,128)(2,1)S(1)} %bitcast.305), channel_id=1, replica_groups=mesh['dp'=4,'gx'=2,'gy'=4] {'gx','gy'}, dimensions={0}, use_global_device_ids=true | all-gather | bytes 737280 | tf_op jit(solution)/shard_map/all_gather | solution.py:249
  150.9 15.8 %all_gather.33 = bf16[512,960]{0,1:T(8,128)(2,1)S(1)} all-gather(bf16[128,960]{0,1:T(8,128)(2,1)S(1)} %bitcast.286), channel_id=1, replica_groups=mesh['dp'=4,'gx'=2,'gy'=4] {'gy'}, dimensions={0}, use_global_device_ids=true | all-gather | bytes 1228800 | tf_op jit(solution)/shard_map/all_gather | solution.py:100
  166.8 12.2 %all_to_all.259 = bf16[512,2,480]{0,2,1:T(8,128)(2,1)S(1)} all-to-all(bf16[512,2,480]{0,2,1:T(8,128)(2,1)S(1)} %bitcast.270), channel_id=1, replica_groups=mesh['dp'=4,'gx'=2,'gy'=4] {'gx'}, dimensions={1} | all-to-all | bytes 1966080 | tf_op jit(solution)/shard_map/all_to_all | solution.py:101
  178.9 3.4 all-to-all-start.8
  184.8 4.1 all-to-all-done.8
  189.0 10.1 %all_gather.36 = bf16[1024,240]{0,1:T(8,128)(2,1)S(1)} all-gather(bf16[512,240]{0,1:T(8,128)(2,1)S(1)} %copy_bitcast_fusion.6), channel_id=1, replica_groups=mesh['dp'=4,'gx'=2,'gy'=4] {'gx'}, dimensions={0}, use_global_device_ids=true | all-gather | bytes 737280 | tf_op jit(solution)/shard_map/all_gather | solution.py:117
  200.3 2.5 convolution_convert_fusion.1
  203.9 16.9 %all_to_all.260 = bf16[4,128,240]{1,2,0:T(8,128)(2,1)S(1)} all-to-all(bf16[4,128,240]{1,2,0:T(8,128)(2,1)S(1)} %copy_bitcast_fusion.11), channel_id=1, replica_groups=mesh['dp'=4,'gx'=2,'gy'=4] {'gy'}, dimensions={0} | all-to-all | bytes 491520 | tf_op jit(solution)/shard_map/all_to_all | solution.py:111
  221.9 38.4 %all_gather.34 = bf16[512,960]{0,1:T(8,128)(2,1)} all-gather(bf16[128,960]{0,1:T(8,128)(2,1)S(1)} %get-tuple-element.79), channel_id=1, replica_groups=mesh['dp'=4,'gx'=2,'gy'=4] {'gy'}, dimensions={0}, use_global_device_ids=true | all-gather | bytes 1228800 | tf_op jit(solution)/shard_map/all_gather | solution.py:100
  260.2 3.6 all-to-all-start.4
  268.0 4.8 all-to-all-done.4
  273.9 4.5 convolution_convert_fusion
  280.6 3.5 all-to-all-start.9
  284.1 42.4 %reduce-scatter.19.cloned.1.call-done = bf16[512,1280]{1,0:T(8,128)(2,1)} async-done(((bf16[1024,1280]{1,0:T(8,128)(2,1)}), bf16[512,1280]{1,0:T(8,128)(2,1)}) %reduce-scatter.19.cloned.1.call-update) | async-done | bytes 1310736 | tf_op jit(solution)/shard_map/reduce_scatter | solution.py:105
  326.5 2.5 copy.97
  329.8 9.9 %all-to-all-start.5 = ((bf16[4,128,1280]{1,2,0:T(8,128)(2,1)}), bf16[4,128,1280]{1,2,0:T(8,128)(2,1)S(1)}, u32[]{:S(2)}, u32[]{:S(2)}) async-start(bf16[4,128,1280]{1,2,0:T(8,128)(2,1)} %copy.97), calls=%async_computation.8 | async-start | bytes 2621440 | tf_op jit(solution)/shard_map/all_to_all | solution.py:111
  339.7 2.2 convert_element_type.331
  342.0 29.2 %all-to-all-done.5 = bf16[4,128,1280]{1,2,0:T(8,128)(2,1)S(1)} async-done(((bf16[4,128,1280]{1,2,0:T(8,128)(2,1)}), bf16[4,128,1280]{1,2,0:T(8,128)(2,1)S(1)}, u32[]{:S(2)}, u32[]{:S(2)}) %all-to-all-start.5) | async-done | bytes 1310752 | tf_op jit(solution)/shard_map/all_to_all | solution.py:111
  373.2 34.1 %all_to_all.261 = bf16[128,4,1280]{0,2,1:T(8,128)(2,1)} all-to-all(bf16[128,4,1280]{0,2,1:T(8,128)(2,1)S(1)} %pad_maximum_fusion), channel_id=1, replica_groups=mesh['dp'=4,'gx'=2,'gy'=4] {'gy'}, dimensions={1} | all-to-all | bytes 2621440 | tf_op jit(solution)/shard_map/all_to_all | solution.py:116
  407.3 2.5 copy.103
  409.9 36.8 %all-gather.5.cloned.1.call-done = bf16[1024,1280]{1,0:T(8,128)(2,1)} async-done(((bf16[512,1280]{1,0:T(8,128)(2,1)}), bf16[1024,1280]{1,0:T(8,128)(2,1)}) %all-gather.5.cloned.1.call-update) | async-done | bytes 2621456 | tf_op jit(solution)/shard_map/all_gather | solution.py:117
  448.6 3.7 convolution_convert_fusion.6
  452.3 26.4 %reduce-scatter.25.cloned.1.call-done = bf16[256,480]{0,1:T(8,128)(2,1)} async-done(((bf16[1024,480]{0,1:T(8,128)(2,1)}), bf16[256,480]{0,1:T(8,128)(2,1)}) %reduce-scatter.25.cloned.1.call-update) | async-done | bytes 245776 | tf_op jit(solution)/shard_map/reduce_scatter | solution.py:129
  479.7 7.6 all_to_all.262
  490.0 9.4 %all_to_all.263 = bf16[128,4,240]{0,2,1:T(8,128)(2,1)S(1)} all-to-all(bf16[128,4,240]{0,2,1:T(8,128)(2,1)S(1)} %bitcast.296), channel_id=1, replica_groups=mesh['dp'=4,'gx'=2,'gy'=4] {'gy'}, dimensions={1} | all-to-all | bytes 491520 | tf_op jit(solution)/shard_map/all_to_all | solution.py:116
  499.4 7.0 all_gather.38
  508.5 2.3 copy.153
  512.9 2.5 convolution_convert_fusion.5
  515.5 24.6 %reduce-scatter.27.cloned.1.call-done = bf16[256,480]{0,1:T(8,128)(2,1)} async-done(((bf16[1024,480]{0,1:T(8,128)(2,1)}), bf16[256,480]{0,1:T(8,128)(2,1)}) %reduce-scatter.27.cloned.1.call-update) | async-done | bytes 245776 | tf_op jit(solution)/shard_map/reduce_scatter | solution.py:129
  541.2 7.6 all_to_all.264
  549.9 5.9 fusion.1
  557.7 2.2 fusion.5
  559.9 2.2 copy.124
  562.2 10.0 %reduce-scatter.33.cloned.1.call-start = ((), (), s32[]{:S(2)}) async-start(), calls=%async_computation.37 | async-start | bytes 884736
  572.2 6.2 fusion.6
  578.4 2.2 copy.126
  582.1 2.9 convolution_multiply_fusion
  585.1 38.2 %reduce-scatter.31.cloned.1.call-done = bf16[128,320]{1,0:T(8,128)(2,1)} async-done(((bf16[1024,320]{1,0:T(8,128)(2,1)}), bf16[128,320]{1,0:T(8,128)(2,1)}) %reduce-scatter.31.cloned.1.call-update) | async-done | bytes 81936
  624.3 65.2 %reduce-scatter.33.cloned.1.call-done = bf16[128,320]{1,0:T(8,128)(2,1)} async-done(((bf16[1024,320]{1,0:T(8,128)(2,1)}), bf16[128,320]{1,0:T(8,128)(2,1)}) %reduce-scatter.33.cloned.1.call-update) | async-done | bytes 81936
  690.6 23.7 %all_to_all.265 = bf16[128,4,400]{0,2,1:T(8,128)(2,1)S(1)} all-to-all(bf16[128,4,400]{0,2,1:T(8,128)(2,1)S(1)} %pad_maximum_fusion.2), channel_id=1, replica_groups=mesh['dp'=4,'gx'=2,'gy'=4] {'gy'}, dimensions={1} | all-to-all | bytes 819200 | tf_op jit(solution)/shard_map/all_to_all | solution.py:116
  714.3 8.6 all_gather.39
  724.4 2.9 copy.152
  727.3 3.2 reshape.297
  730.5 2.8 convolution_convert_fusion.4
  733.3 15.8 %all-gather.3.cloned.1.call-done = bf16[512,2560]{0,1:T(8,128)(2,1)} async-done(((bf16[128,2560]{0,1:T(8,128)(2,1)}), bf16[512,2560]{0,1:T(8,128)(2,1)}) %all-gather.3.cloned.1.call-update) | async-done | bytes 2621456 | tf_op jit(solution)/shard_map/all_gather | solution.py:100
  749.1 4.4 copy.98
  753.5 5.2 all-to-all-start.6
  758.8 3.2 convolution_convert_fusion.2
  763.1 26.4 %all-to-all-done.6 = bf16[512,2,1280]{2,0,1:T(8,128)(2,1)} async-done(((bf16[512,2,1280]{2,0,1:T(8,128)(2,1)}), bf16[512,2,1280]{2,0,1:T(8,128)(2,1)}, u32[]{:S(2)}, u32[]{:S(2)}) %all-to-all-start.6) | async-done | bytes 2621472 | tf_op jit(solution)/shard_map/all_to_all | solution.py:101
  789.5 3.4 convolution_convert_fusion.8
  793.1 3.5 convolution_convert_fusion.3
  801.5 3.4 all-to-all-start.15
  808.1 60.1 %all-reduce.4.cloned.1.call-done = (bf16[480,240]{0,1:T(8,128)(2,1)}, bf16[480,80]{0,1:T(8,128)(2,1)}, bf16[480,80]{0,1:T(8,128)(2,1)}, bf16[480,240]{1,0:T(8,12...) async-done(((bf16[480,240]{0,1:T(8,128)(2,1)}, bf16[480,80]{0,1:T(8,128)(2,1)}, bf16[480,80]{0,1:T(8,128)(2,1)}, ...) | async-done | bytes 2457616 | tf_op jit(solution)/shard_map/psum | solution.py:309
  868.2 2.3 convert_element_type.316
  870.5 2.2 convert_element_type.317
  876.9 4.6 all-to-all-start.7
  881.9 40.0 %all-reduce = (f32[960]{0:T(1024)}, f32[960]{0:T(1024)}) all-reduce(f32[960]{0:T(1024)S(1)} %get-tuple-element.55, f32[960]{0:T(1024)S(1)} %get-tuple-element.57), channel_id=1, replica_groups=mesh['dp'=4,'gx'=2,'gy'=4] {'dp','gx','gy'}, use_global_device_ids=true, to_apply=%region_25.26 | all-reduce | flops 1920 | bytes 15360 | tf_op jit(solution)/shard_map/psum | solution.py:307
  (189 shorter events, 64.2 us)
Async XLA Ops:
  7.2 193.1 %copy-start = (bf16[1280,240]{0,1:T(8,128)(2,1)S(1)}, bf16[1280,240]{0,1:T(8,128)(2,1)}, u32[]{:S(2)}) copy-start(bf16[1280,240]{0,1:T(8,128)(2,1)} %param.22) | copy-start | bytes 1843204
  7.2 29.0 %copy-start.29 = (bf16[480,80]{0,1:T(8,128)(2,1)S(1)}, bf16[480,80]{0,1:T(8,128)(2,1)}, u32[]{:S(2)}) copy-start(bf16[480,80]{0,1:T(8,128)(2,1)} %param.16) | copy-start | bytes 230404
  7.2 29.2 %copy-start.30 = (bf16[480,80]{0,1:T(8,128)(2,1)S(1)}, bf16[480,80]{0,1:T(8,128)(2,1)}, u32[]{:S(2)}) copy-start(bf16[480,80]{0,1:T(8,128)(2,1)} %param.17) | copy-start | bytes 230404
  9.5 39.6 %copy-start.36 = (bf16[480,240]{1,0:T(8,128)(2,1)S(1)}, bf16[480,240]{1,0:T(8,128)(2,1)}, u32[]{:S(2)}) copy-start(bf16[480,240]{1,0:T(8,128)(2,1)} %param.15) | copy-start | bytes 691204
  32.6 15.5 %all-to-all-start = ((bf16[512,2,480]{0,2,1:T(8,128)(2,1)}), bf16[512,2,480]{0,2,1:T(8,128)(2,1)S(1)}, u32[]{:S(2)}, u32[]{:S(2)}) async-start(bf16[512,2,480]{0,2,1:T(8,128)(2,1)} %bitcast), calls=%async_computation | async-start | bytes 1966080 | tf_op jit(solution)/shard_map/all_to_all | solution.py:101
  36.2 31.8 %reduce-scatter.15.cloned.1.call-start = ((), (), s32[]{:S(2)}) async-start(), calls=%async_computation.26 | async-start | bytes 1228800 | tf_op jit(solution)/shard_map/reduce_scatter | solution.py:105
  36.4 14.5 %copy-start.25 = (bf16[480,80]{1,0:T(8,128)(2,1)}, bf16[480,80]{1,0:T(8,128)(2,1)S(1)}, u32[]{:S(2)}) copy-start(bf16[480,80]{1,0:T(8,128)(2,1)S(1)} %copy.90) | copy-start | bytes 230404
  36.5 14.3 %copy-start.27 = (bf16[480,80]{1,0:T(8,128)(2,1)}, bf16[480,80]{1,0:T(8,128)(2,1)S(1)}, u32[]{:S(2)}) copy-start(bf16[480,80]{1,0:T(8,128)(2,1)S(1)} %copy.91) | copy-start | bytes 230404
  48.2 1.0 copy-start.15
  49.2 25.3 %copy-start.35 = (s32[1024]{0:T(1024)S(1)}, s32[1024]{0:T(1024)}, u32[]{:S(2)}) copy-start(s32[1024]{0:T(1024)} %param.13) | copy-start | bytes 12292
  69.8 16.5 %all-to-all-start.1 = ((bf16[4,128,400]{1,2,0:T(8,128)(2,1)}), bf16[4,128,400]{1,2,0:T(8,128)(2,1)S(1)}, u32[]{:S(2)}, u32[]{:S(2)}) async-start(bf16[4,128,400]{1,2,0:T(8,128)(2,1)} %copy_bitcast_fusion.4), calls=%async_computation.2 | async-start | bytes 819200 | tf_op jit(solution)/shard_map/all_to_all | solution.py:111
  115.6 1.3 copy-start.9
  116.9 32.1 %copy-start.1 = (f32[5,1024,128,3]{2,1,3,0:T(8,128)}, f32[5,1024,128,3]{2,1,3,0:T(8,128)S(1)}, u32[]{:S(2)}) copy-start(f32[5,1024,128,3]{2,1,3,0:T(8,128)S(1)} %get-tuple-element.91) | copy-start | bytes 23592964
  149.0 1.9 copy-start.21
  150.9 15.8 %copy-start.14 = (bf16[5,64,3,128]{3,1,2,0:T(8,128)(2,1)}, bf16[5,64,3,128]{3,1,2,0:T(8,128)(2,1)S(1)}, u32[]{:S(2)}) copy-start(bf16[5,64,3,128]{3,1,2,0:T(8,128)(2,1)S(1)} %convolution_convert_fusion.12) | copy-start | bytes 737284
  150.9 32.6 %copy-start.19 = (bf16[480,240]{1,0:T(8,128)(2,1)S(1)}, bf16[480,240]{1,0:T(8,128)(2,1)}, u32[]{:S(2)}) copy-start(bf16[480,240]{1,0:T(8,128)(2,1)} %param.18) | copy-start | bytes 691204
  178.9 10.0 %all-to-all-start.8 = ((bf16[128,4,240]{0,2,1:T(8,128)(2,1)}), bf16[128,4,240]{0,2,1:T(8,128)(2,1)S(1)}, u32[]{:S(2)}, u32[]{:S(2)}) async-start(bf16[128,4,240]{0,2,1:T(8,128)(2,1)} %bitcast.34), calls=%async_computation.12 | async-start | bytes 491520 | tf_op jit(solution)/shard_map/all_to_all | solution.py:116
  182.3 20.5 %reduce-scatter.17.cloned.1.call-start = ((), (), s32[]{:S(2)}) async-start(), calls=%async_computation.27 | async-start | bytes 737280 | tf_op jit(solution)/shard_map/reduce_scatter | solution.py:105
  182.5 1.0 copy-start.4
  184.8 93.7 %reduce-scatter.23.cloned.1.call-start = ((), (), s32[]{:S(2)}) async-start(), calls=%async_computation.31 | async-start | bytes 3276800 | tf_op jit(solution)/shard_map/reduce_scatter | solution.py:129
  199.0 0.9 copy-start.11
  202.7 18.1 %copy-start.3 = (bf16[128,960]{0,1:T(8,128)(2,1)S(1)}, bf16[128,960]{0,1:T(8,128)(2,1)}, u32[]{:S(2)}) copy-start(bf16[128,960]{0,1:T(8,128)(2,1)} %param.12) | copy-start | bytes 737284
  202.7 18.2 %copy-start.33 = (f32[960]{0:T(1024)S(1)}, f32[960]{0:T(1024)}, u32[]{:S(2)}) copy-start(f32[960]{0:T(1024)} %param.19) | copy-start | bytes 11524
  260.2 12.6 %all-to-all-start.4 = ((bf16[512,2,480]{0,2,1:T(8,128)(2,1)}), bf16[512,2,480]{0,2,1:T(8,128)(2,1)S(1)}, u32[]{:S(2)}, u32[]{:S(2)}) async-start(bf16[512,2,480]{0,2,1:T(8,128)(2,1)} %bitcast.268), calls=%async_computation.6 | async-start | bytes 1966080 | tf_op jit(solution)/shard_map/all_to_all | solution.py:101
  263.8 62.7 %reduce-scatter.19.cloned.1.call-start = ((), (), s32[]{:S(2)}) async-start(), calls=%async_computation.28 | async-start | bytes 3932160 | tf_op jit(solution)/shard_map/reduce_scatter | solution.py:105
  273.0 1.0 copy-start.17
  280.6 48.4 %all-to-all-start.9 = ((bf16[2,128,1280]{1,2,0:T(8,128)(2,1)}), bf16[2,128,1280]{1,2,0:T(8,128)(2,1)S(1)}, u32[]{:S(2)}, u32[]{:S(2)}) async-start(bf16[2,128,1280]{1,2,0:T(8,128)(2,1)} %copy.102), calls=%async_computation.14 | async-start | bytes 1310720 | tf_op jit(solution)/shard_map/all_to_all | solution.py:132
  329.0 0.8 copy-start.8
  329.8 41.3 %all-to-all-start.5 = ((bf16[4,128,1280]{1,2,0:T(8,128)(2,1)}), bf16[4,128,1280]{1,2,0:T(8,128)(2,1)S(1)}, u32[]{:S(2)}, u32[]{:S(2)}) async-start(bf16[4,128,1280]{1,2,0:T(8,128)(2,1)} %copy.97), calls=%async_computation.8 | async-start | bytes 2621440 | tf_op jit(solution)/shard_map/all_to_all | solution.py:111
  339.7 106.9 %all-gather.5.cloned.1.call-start = ((), (), s32[]{:S(2)}) async-start(), calls=%async_computation.32 | async-start | bytes 3932160 | tf_op jit(solution)/shard_map/all_gather | solution.py:117
  409.8 68.9 %reduce-scatter.25.cloned.1.call-start = ((), (), s32[]{:S(2)}) async-start(), calls=%async_computation.33 | async-start | bytes 1228800 | tf_op jit(solution)/shard_map/reduce_scatter | solution.py:129
  452.3 87.9 %reduce-scatter.27.cloned.1.call-start = ((), (), s32[]{:S(2)}) async-start(), calls=%async_computation.34 | async-start | bytes 1228800 | tf_op jit(solution)/shard_map/reduce_scatter | solution.py:129
  515.5 107.8 %reduce-scatter.31.cloned.1.call-start = ((), (), s32[]{:S(2)}) async-start(), calls=%async_computation.36 | async-start | bytes 884736
  548.8 7.0 copy-start.20
  549.9 7.8 copy-start.10
  555.8 1.9 copy-start.2
  562.2 127.3 %reduce-scatter.33.cloned.1.call-start = ((), (), s32[]{:S(2)}) async-start(), calls=%async_computation.37 | async-start | bytes 884736
  580.7 168.4 %all-gather.3.cloned.1.call-start = ((), (), s32[]{:S(2)}) async-start(), calls=%async_computation.29 | async-start | bytes 3276800 | tf_op jit(solution)/shard_map/all_gather | solution.py:100
  582.0 217.8 %reduce-scatter.29.cloned.1.call-start = ((), (), s32[]{:S(2)}) async-start(), calls=%async_computation.35 | async-start | bytes 1228800 | tf_op jit(solution)/shard_map/reduce_scatter | solution.py:129
  722.9 10.4 %copy-start.6 = (bf16[1024,400]{0,1:T(8,128)(2,1)}, bf16[1024,400]{0,1:T(8,128)(2,1)S(1)}, u32[]{:S(2)}) copy-start(bf16[1024,400]{0,1:T(8,128)(2,1)S(1)} %all_gather.39) | copy-start | bytes 2457604
  722.9 7.6 copy-start.26
  722.9 7.6 copy-start.28
  722.9 7.6 copy-start.37
  753.5 5.2 copy-start.18
  753.5 36.0 %all-to-all-start.6 = ((bf16[512,2,1280]{2,0,1:T(8,128)(2,1)}), bf16[512,2,1280]{2,0,1:T(8,128)(2,1)}, u32[]{:S(2)}, u32[]{:S(2)}) async-start(bf16[512,2,1280]{2,0,1:T(8,128)(2,1)} %copy.98), calls=%async_computation.9 | async-start | bytes 5242880 | tf_op jit(solution)/shard_map/all_to_all | solution.py:101
  758.7 47.8 %reduce-scatter.21.cloned.1.call-start = ((), (), s32[]{:S(2)}) async-start(), calls=%async_computation.30 | async-start | bytes 737280 | tf_op jit(solution)/shard_map/reduce_scatter | solution.py:105
  789.5 3.5 copy-start.12
  793.0 3.6 copy-start.5
  793.0 3.6 copy-start.13
  793.0 75.2 %all-reduce.4.cloned.1.call-start = ((), (), s32[]{:S(2)}) async-start(), calls=%async_computation.38 | async-start | bytes 4997120 | tf_op jit(solution)/shard_map/psum | solution.py:309
  793.1 4.7 copy-start.7
  793.1 4.7 copy-start.16
  801.5 75.4 %all-to-all-start.15 = ((bf16[2,128,480]{1,2,0:T(8,128)(2,1)}), bf16[2,128,480]{1,2,0:T(8,128)(2,1)S(1)}, u32[]{:S(2)}, u32[]{:S(2)}) async-start(bf16[2,128,480]{1,2,0:T(8,128)(2,1)} %copy_bitcast_fusion.7), calls=%async_computation.23 | async-start | bytes 491520 | tf_op jit(solution)/shard_map/all_to_all | solution.py:132
  868.2 4.5 copy-start.22
  868.2 5.6 copy-start.24
  870.5 4.2 copy-start.23
  870.5 5.1 copy-start.32
  870.5 5.8 copy-start.31
  872.7 8.9 copy-start.34
  876.9 45.0 %all-to-all-start.7 = ((bf16[4,128,240]{1,2,0:T(8,128)(2,1)}), bf16[4,128,240]{1,2,0:T(8,128)(2,1)S(1)}, u32[]{:S(2)}, u32[]{:S(2)}) async-start(bf16[4,128,240]{1,2,0:T(8,128)(2,1)} %copy_bitcast_fusion.10), calls=%async_computation.11 | async-start | bytes 491520 | tf_op jit(solution)/shard_map/all_to_all | solution.py:111
Sparse Core Ops, SparseCore 0:
  51.0 16.9 reduce-scatter.14
  186.0 16.1 reduce-scatter.16
  204.5 67.8 reduce-scatter.22
  278.5 47.9 reduce-scatter.18
  409.9 36.6 all-gather.4
  452.4 26.2 reduce-scatter.24
  515.6 24.5 reduce-scatter.26
  562.3 60.9 reduce-scatter.30
  627.1 62.2 reduce-scatter.32
  690.9 58.1 all-gather.2
  752.0 25.4 reduce-scatter.28
  793.1 13.2 reduce-scatter.20
  809.9 58.2 all-reduce.3
where the time goes:
time: 942 us; the launch traced here: 931 us
  waiting for transfers between devices  416 us (44%)
  blocking collectives  314 us (33%)
  local copies, waits for them, and re-layouts  57.4 us (6%)
  starting transfers between devices  52.5 us (6%)
  matrix products  51.3 us (5%)
  other arithmetic  25.4 us (3%)
  between operations  14.8 us (2%)
    unnamed x15, waiting for transfers between devices  104 us
    all_gather x3, blocking collectives, spread(): stacked = lax.all_gather(local_rows, 'gy', axis=0, tiled=True)  77.2 us
    all_to_all x3, blocking collectives, spread_grads(): lax.all_to_all(pack_columns(parts), 'gy', split_axis=1, concat_axis=0, ti...  67.1 us
    reduce_scatter x4, waiting for transfers between devices, collect(): lax.psum_scatter(jnp.dot(spread_inputs, weight, preferred_element_type=jn...  61 us
    psum x1, waiting for transfers between devices, on_device(): lax.psum(query_grad.astype(jnp.bfloat16), 'dp').astype(jnp.float32)  60.1 us
    reduce_scatter x4, waiting for transfers between devices, gather_inputs(): lax.psum_scatter(back_product(reordered, weight).astype(jnp.bfloat16), 'g...  51 us
    all_to_all x3, waiting for transfers between devices, spread(): lax.all_to_all(stacked, 'gx', split_axis=1, concat_axis=0, tiled=True)  42.8 us
    all_to_all x3, waiting for transfers between devices, collect(): lax.all_to_all(summed, 'gy', split_axis=0, concat_axis=1, tiled=True)  40.6 us
  transfers between devices with their start and end apart: 22, of which 16 were waited for; matrix products, arithmetic and copies ran while one was open for 9% of the time, Pallas kernels for 0%

commit v1 on v0

--- a/solution.py
+++ b/solution.py
@@ -77,61 +77,36 @@
     )
 
 
-def pack_columns(parts):
-    fanout = lax.axis_size("gy")
-    count_of_rows = parts[0].shape[0]
-    blocks = [column_part.reshape(count_of_rows, fanout, -1) for column_part in parts]
-    return jnp.concatenate(blocks, axis=2).reshape(count_of_rows, -1)
-
-
-def unpack_columns(packed, widths):
-    fanout = lax.axis_size("gy")
-    count_of_rows = packed.shape[0]
-    shaped = packed.reshape(count_of_rows, fanout, -1)
-    outputs = []
-    offset = 0
-    for block_width in widths:
-        outputs.append(shaped[:, :, offset : offset + block_width].reshape(count_of_rows, -1))
-        offset = offset + block_width
-    return outputs
-
-
-def spread(local_rows):
-    stacked = lax.all_gather(local_rows, "gy", axis=0, tiled=True)
-    return lax.all_to_all(stacked, "gx", split_axis=1, concat_axis=0, tiled=True)
-
-
-def collect(spread_inputs, weight, widths):
-    summed = lax.psum_scatter(
-        jnp.dot(spread_inputs, weight, preferred_element_type=jnp.float32).astype(jnp.bfloat16),
-        "gx",
-        scatter_dimension=0,
-        tiled=True,
-    )
-    moved = lax.all_to_all(summed, "gy", split_axis=0, concat_axis=1, tiled=True)
-    return unpack_columns(moved, widths)
-
-
-def spread_grads(parts):
-    moved = lax.all_to_all(pack_columns(parts), "gy", split_axis=1, concat_axis=0, tiled=True)
-    return lax.all_gather(moved, "gx", axis=0, tiled=True)
-
-
-def gather_inputs(full_grads, weight):
+def gather_blocks(block):
+    return lax.all_gather(block, ("gx", "gy"), axis=0, tiled=False)
+
+
+def whole_weight(blocks):
     fanin = lax.axis_size("gx")
     fanout = lax.axis_size("gy")
-    count_of_rows = full_grads.shape[0] // (fanin * fanout)
-    reordered = (
-        full_grads.reshape(fanin, fanout, count_of_rows, -1)
-        .transpose(1, 0, 2, 3)
-        .reshape(fanin * fanout * count_of_rows, -1)
-    )
-    summed = lax.psum_scatter(
-        back_product(reordered, weight).astype(jnp.bfloat16), "gy", scatter_dimension=0, tiled=True
-    ).astype(jnp.float32)
-    return lax.all_to_all(
-        summed.astype(jnp.bfloat16), "gx", split_axis=0, concat_axis=1, tiled=True
-    ).astype(summed.dtype)
+    rows, columns = blocks.shape[1:]
+    shaped = blocks.reshape(fanin, fanout, rows, columns).transpose(0, 2, 1, 3)
+    return shaped.reshape(fanin * rows, fanout * columns)
+
+
+def cut_blocks(grad):
+    fanin = lax.axis_size("gx")
+    fanout = lax.axis_size("gy")
+    rows, columns = grad.shape[0] // fanin, grad.shape[1] // fanout
+    shaped = grad.astype(jnp.bfloat16).reshape(fanin, rows, fanout, columns).transpose(0, 2, 1, 3)
+    return shaped.reshape(fanin * fanout, rows, columns)
+
+
+def scatter_blocks(blocks):
+    return lax.psum_scatter(blocks, ("gx", "gy"), scatter_dimension=0, tiled=False)
+
+
+def hidden_slice(weight, groups):
+    rows, columns = weight.shape
+    share = rows // groups // lax.axis_size("dp")
+    shaped = weight.reshape(groups, lax.axis_size("dp"), share, columns)
+    picked = lax.dynamic_slice_in_dim(shaped, lax.axis_index("dp"), 1, 1)
+    return picked.reshape(groups * share, columns)
 
 
 def head_views(rotated_query, key_sequence, value_sequence):
@@ -225,7 +200,9 @@
     cotangent,
 ):
     count_of_rows = inputs.shape[0]
+    fanin = lax.axis_size("gx")
     fanout = lax.axis_size("gy")
+    replicas = lax.axis_size("dp")
     begin_row = (lax.axis_index("gx") * fanout + lax.axis_index("gy")) * count_of_rows
     seq_begin = begin_row // SEQUENCE_LENGTH * SEQUENCE_LENGTH
     local_places = begin_row - seq_begin + jnp.arange(count_of_rows)
@@ -236,84 +213,147 @@
     )
     residual = inputs.astype(jnp.float32)
     rms_one, unit_one, normed_one = normalize(residual, attn_gain)
-    spread_one = spread(normed_one)
-    attn_weight = jnp.concatenate([query_weight, key_weight, value_weight], axis=1)
-    attn_widths = [query_weight.shape[1], key_weight.shape[1], value_weight.shape[1]]
-    query_rows, key_rows, value_row_list = collect(spread_one, attn_weight, attn_widths)
+
+    q_width, k_width, v_width = query_weight.shape[1], key_weight.shape[1], value_weight.shape[1]
+    packed = jnp.concatenate([query_weight, key_weight, value_weight, output_weight], axis=1)
+    attn_blocks = gather_blocks(packed)
+    query_full = whole_weight(attn_blocks[:, :, :q_width])
+    key_full = whole_weight(attn_blocks[:, :, q_width : q_width + k_width])
+    value_full = whole_weight(attn_blocks[:, :, q_width + k_width : q_width + k_width + v_width])
+    output_full = whole_weight(attn_blocks[:, :, q_width + k_width + v_width :])
+
+    groups = fanout // fanin
+    gate_part = hidden_slice(gate_weight.T, 1)
+    up_part = hidden_slice(up_weight.T, 1)
+    down_part = hidden_slice(down_weight, groups)
+    share = gate_part.shape[0]
+    gate_up_blocks = gather_blocks(jnp.concatenate([gate_part, up_part], axis=0))
+    down_blocks = gather_blocks(down_part)
+    model_block = gate_part.shape[1]
+    gate_up_rows = (
+        gate_up_blocks.reshape(fanin, fanout, 2, share, model_block)
+        .transpose(2, 1, 3, 0, 4)
+        .reshape(2 * fanout * share, fanin * model_block)
+    )
+    hidden_width = fanout * share
+    down_rows = whole_weight(down_blocks)
+
+    query_rows = jnp.dot(normed_one, query_full, preferred_element_type=jnp.float32).astype(jnp.bfloat16)
+    key_rows = jnp.dot(normed_one, key_full, preferred_element_type=jnp.float32).astype(jnp.bfloat16)
+    value_rows = jnp.dot(normed_one, value_full, preferred_element_type=jnp.float32).astype(jnp.bfloat16)
     rotated_query = rotate(query_rows.astype(jnp.float32), cos_table, sin_table).astype(
         jnp.bfloat16
     )
     rotated_key = rotate(key_rows.astype(jnp.float32), cos_table, sin_table).astype(jnp.bfloat16)
-    key_all, value_all = (
-        lax.all_gather(rotated_key, ("gx", "gy"), axis=0, tiled=True),
-        lax.all_gather(value_row_list, ("gx", "gy"), axis=0, tiled=True),
-    )
+    kv_all = lax.all_gather(
+        jnp.concatenate([rotated_key, value_rows], axis=1), ("gx", "gy"), axis=0, tiled=True
+    )
+    kv_width = rotated_key.shape[1]
+    key_all, value_all = kv_all[:, :kv_width], kv_all[:, kv_width:]
     attention_mixture, logsum = attend(rotated_query, key_all, value_all, allowed)
-    mixed_spread = spread(attention_mixture)
-    attn_out = collect(mixed_spread, output_weight, [output_weight.shape[1]])[0]
+    attn_out = jnp.dot(attention_mixture, output_full, preferred_element_type=jnp.float32).astype(
+        jnp.bfloat16
+    )
     hidden = residual + attn_out.astype(jnp.float32)
     rms_two, unit_two, normed_two = normalize(hidden, mlp_gain)
-    spread_two = spread(normed_two)
-    mlp_weight = jnp.concatenate([gate_weight, up_weight], axis=1)
-    gate_width = gate_weight.shape[1]
-    gate_rows, up_rows = collect(spread_two, mlp_weight, [gate_width, up_weight.shape[1]])
-    gate_float = gate_rows.astype(jnp.float32)
-    up_float = up_rows.astype(jnp.float32)
+
+    cot_all = lax.all_gather(cotangent, "dp", axis=0, tiled=True)
+    normed_all = lax.all_gather(normed_two, "dp", axis=0, tiled=True)
+    gate_up = back_product(normed_all, gate_up_rows).astype(jnp.bfloat16)
+    gate_float = gate_up[:, :hidden_width].astype(jnp.float32)
+    up_float = gate_up[:, hidden_width:].astype(jnp.float32)
     sigmoid_gate = jax.nn.sigmoid(gate_float)
     activated = (gate_float * sigmoid_gate * up_float).astype(jnp.bfloat16)
-    act_spread = spread(activated)
-    mlp_out = collect(act_spread, down_weight, [down_weight.shape[1]])[0]
-    layer_out = (hidden + mlp_out.astype(jnp.float32)).astype(jnp.bfloat16)
-    cot_spread = spread_grads([cotangent])
-    down_grad = weight_product(act_spread, cot_spread)
-    dactivated = gather_inputs(cot_spread, down_weight)
+    dactivated = back_product(cot_all, down_rows)
     gate_delta = (
         dactivated * up_float * sigmoid_gate * (1.0 + gate_float * (1.0 - sigmoid_gate))
     ).astype(jnp.bfloat16)
     up_delta = (dactivated * gate_float * sigmoid_gate).astype(jnp.bfloat16)
-    mlp_spread_grads = spread_grads([gate_delta, up_delta])
-    mlp_grads = weight_product(spread_two, mlp_spread_grads)
-    gate_grad = mlp_grads[:, :gate_width]
-    up_grad = mlp_grads[:, gate_width:]
-    dnormed_two = gather_inputs(mlp_spread_grads, mlp_weight)
+    deltas = jnp.concatenate([gate_delta, up_delta], axis=1)
+    dnormed_two = lax.psum_scatter(
+        jnp.dot(deltas, gate_up_rows, preferred_element_type=jnp.float32).astype(jnp.bfloat16),
+        "dp",
+        scatter_dimension=0,
+        tiled=True,
+    ).astype(jnp.float32)
+    mlp_out = lax.psum_scatter(
+        jnp.dot(activated, down_rows, preferred_element_type=jnp.float32).astype(jnp.bfloat16),
+        "dp",
+        scatter_dimension=0,
+        tiled=True,
+    )
+    layer_out = (hidden + mlp_out.astype(jnp.float32)).astype(jnp.bfloat16)
+
+    gate_up_grad = (
+        weight_product(deltas, normed_all)
+        .astype(jnp.bfloat16)
+        .reshape(2, fanout, share, fanin, model_block)
+        .transpose(3, 1, 0, 2, 4)
+        .reshape(fanin * fanout, 2 * share, model_block)
+    )
+    down_grad_blocks = cut_blocks(weight_product(activated, cot_all))
+    if groups * share == 2 * share:
+        mlp_sum = scatter_blocks(jnp.concatenate([gate_up_grad, down_grad_blocks], axis=2))
+        mlp_sum = lax.all_gather(mlp_sum, "dp", axis=0, tiled=False)
+        gate_up_sum, down_sum = mlp_sum[:, :, :model_block], mlp_sum[:, :, model_block:]
+    else:
+        gate_up_sum = lax.all_gather(scatter_blocks(gate_up_grad), "dp", axis=0, tiled=False)
+        down_sum = lax.all_gather(scatter_blocks(down_grad_blocks), "dp", axis=0, tiled=False)
+    gate_grad = gate_up_sum[:, :share].reshape(replicas * share, model_block).T.astype(jnp.float32)
+    up_grad = gate_up_sum[:, share:].reshape(replicas * share, model_block).T.astype(jnp.float32)
+    down_grad = (
+        down_sum.reshape(replicas, groups, share, -1)
+        .transpose(1, 0, 2, 3)
+        .reshape(down_weight.shape)
+        .astype(jnp.float32)
+    )
+
     dhidden_norm, mlpgain_part = normalize_back(dnormed_two, mlp_gain, rms_two, unit_two)
     dhidden = cotangent.astype(jnp.float32) + dhidden_norm
     dhidden_bf = dhidden.astype(jnp.bfloat16)
-    hidden_spread = spread_grads([dhidden_bf])
-    output_grad = weight_product(mixed_spread, hidden_spread)
-    mixture_gradient = gather_inputs(hidden_spread, output_weight).astype(jnp.bfloat16)
+    output_sum = scatter_blocks(cut_blocks(weight_product(attention_mixture, dhidden_bf)))
+    mixture_gradient = back_product(dhidden_bf, output_full).astype(jnp.bfloat16)
     dquery_rot, dkey_seq, dvalue_seq = attend_back(
         rotated_query, key_all, value_all, allowed, logsum, attention_mixture, mixture_gradient
     )
-    dkey_rot, dvalue_rows = (
-        lax.psum_scatter(
-            dkey_seq.astype(jnp.bfloat16), ("gx", "gy"), scatter_dimension=0, tiled=True
-        ).astype(jnp.float32),
-        lax.psum_scatter(
-            dvalue_seq.astype(jnp.bfloat16), ("gx", "gy"), scatter_dimension=0, tiled=True
-        ).astype(jnp.float32),
+    dkv = lax.psum_scatter(
+        jnp.concatenate([dkey_seq, dvalue_seq], axis=1).astype(jnp.bfloat16),
+        ("gx", "gy"),
+        scatter_dimension=0,
+        tiled=True,
     )
     dquery = unrotate(dquery_rot, cos_table, sin_table).astype(jnp.bfloat16)
-    dkey = unrotate(dkey_rot, cos_table, sin_table).astype(jnp.bfloat16)
-    dvalue_bf = dvalue_rows.astype(jnp.bfloat16)
-    attn_spread_grads = spread_grads([dquery, dkey, dvalue_bf])
-    attn_grads = weight_product(spread_one, attn_spread_grads)
-    query_grad = attn_grads[:, : attn_widths[0]]
-    key_grad = attn_grads[:, attn_widths[0] : attn_widths[0] + attn_widths[1]]
-    value_grad = attn_grads[:, attn_widths[0] + attn_widths[1] :]
-    dnormed_one = gather_inputs(attn_spread_grads, attn_weight)
+    query_sum = scatter_blocks(cut_blocks(weight_product(normed_one, dquery)))
+    dkey = unrotate(dkv[:, :kv_width].astype(jnp.float32), cos_table, sin_table).astype(jnp.bfloat16)
+    dvalue_bf = dkv[:, kv_width:]
+    kv_sum = scatter_blocks(
+        jnp.concatenate(
+            [
+                cut_blocks(weight_product(normed_one, dkey)),
+                cut_blocks(weight_product(normed_one, dvalue_bf)),
+            ],
+            axis=2,
+        )
+    )
+    dnormed_one = (
+        back_product(dquery, query_full)
+        + back_product(dkey, key_full)
+        + back_product(dvalue_bf, value_full)
+    )
     dresidual, attgain_part = normalize_back(dnormed_one, attn_gain, rms_one, unit_one)
     input_grad = (dhidden + dresidual).astype(jnp.bfloat16)
-    attgain_grad, mlpgain_grad = lax.psum((attgain_part, mlpgain_part), ("dp", "gx", "gy"))
-    query_grad, key_grad, value_grad, output_grad, gate_grad, up_grad, down_grad = (
-        lax.psum(query_grad.astype(jnp.bfloat16), "dp").astype(jnp.float32),
-        lax.psum(key_grad.astype(jnp.bfloat16), "dp").astype(jnp.float32),
-        lax.psum(value_grad.astype(jnp.bfloat16), "dp").astype(jnp.float32),
-        lax.psum(output_grad.astype(jnp.bfloat16), "dp").astype(jnp.float32),
-        lax.psum(gate_grad.astype(jnp.bfloat16), "dp").astype(jnp.float32),
-        lax.psum(up_grad.astype(jnp.bfloat16), "dp").astype(jnp.float32),
-        lax.psum(down_grad.astype(jnp.bfloat16), "dp").astype(jnp.float32),
-    )
+    gain_parts = lax.all_gather(
+        jnp.stack([attgain_part, mlpgain_part]), ("dp", "gx", "gy"), axis=0, tiled=False
+    )
+    attgain_grad, mlpgain_grad = jnp.sum(gain_parts, axis=0)
+    attn_sum = lax.psum(jnp.concatenate([output_sum, query_sum, kv_sum], axis=1), "dp").astype(
+        jnp.float32
+    )
+    o_width = output_weight.shape[1]
+    output_grad = attn_sum[:, :o_width]
+    query_grad = attn_sum[:, o_width : o_width + q_width]
+    key_grad = attn_sum[:, o_width + q_width : o_width + q_width + k_width]
+    value_grad = attn_sum[:, o_width + q_width + k_width :]
     return (
         layer_out,
         input_grad,

time: 942 us -> 800 us (0.85)
  blocking collectives: 314 us -> 89.3 us
  local copies, waits for them, and re-layouts: 57.4 us -> 131 us
  waiting for transfers between devices: 416 us -> 487 us
  starting transfers between devices: 52.5 us -> 1.33 us
    reduce_scatter x8 -> x4, waiting for transfers between devices: 112 us -> 237 us  [scatter_blocks(): lax.psum_scatter(blocks, ('gx', 'gy'), scatter_dimension=0, tiled=False)]
    all_gather x2 -> x5, waiting for transfers between devices: 52.6 us -> 168 us  [the longest x3 158 us: gather_blocks(): return lax.all_gather(block, ('gx', 'gy'), axis=0, tiled=False)]
    all_to_all x7 -> x0, blocking collectives: 111 us -> none  [the longest x3 67.1 us: spread_grads(): lax.all_to_all(pack_columns(parts), 'gy', split_axis=1, concat_axis=0, ti...]
    all_to_all x9 -> x0, waiting for transfers between devices: 87.5 us -> none  [the longest x3 42.8 us: spread(): lax.all_to_all(stacked, 'gx', split_axis=1, concat_axis=0, tiled=True)]
    all_gather x8 -> x3, blocking collectives: 162 us -> 89.3 us  [the longest x1 69.5 us: on_device(): lax.all_gather(jnp.stack([attgain_part, mlpgain_part]), ('dp', 'gx', 'gy'...]
    psum x1, waiting for transfers between devices: 60.1 us -> 0.01 us  [on_device(): lax.psum(jnp.concatenate([output_sum, query_sum, kv_sum], axis=1), 'dp')]
    all_to_all x9 -> x0, starting transfers between devices: 41.8 us -> none  [the longest x3 19.1 us: collect(): lax.all_to_all(summed, 'gy', split_axis=0, concat_axis=1, tiled=True)]
    psum x1 -> x0, blocking collectives: 40 us -> none  [on_device(): lax.psum((attgain_part, mlpgain_part), ('dp', 'gx', 'gy'))]
  transfers between devices with their start and end apart: 22 -> 13, of which waited for: 16 -> 11; matrix products, arithmetic and copies ran while one was open for 9% -> 19% of each run, Pallas kernels for 0% -> 0%
where the time goes in v1:
time: 800 us; the launch traced here: 793 us
  waiting for transfers between devices  487 us (61%)
  local copies, waits for them, and re-layouts  131 us (16%)
  blocking collectives  89.3 us (11%)
  matrix products  48.1 us (6%)
  other arithmetic  21.8 us (3%)
  between operations  14.9 us (2%)
    reduce_scatter x4, waiting for transfers between devices, scatter_blocks(): lax.psum_scatter(blocks, ('gx', 'gy'), scatter_dimension=0, tiled=False)  237 us
    all_gather x3, waiting for transfers between devices, gather_blocks(): return lax.all_gather(block, ('gx', 'gy'), axis=0, tiled=False)  158 us
    unnamed x16, waiting for transfers between devices  81.6 us
    all_gather x1, blocking collectives, on_device(): lax.all_gather(jnp.stack([attgain_part, mlpgain_part]), ('dp', 'gx', 'gy'...  69.5 us
    reshape x6, local copies, waits for them, and re-layouts, cut_blocks(): grad.astype(jnp.bfloat16).reshape(fanin, rows, fanout, columns)  28.6 us
    unnamed x90, local copies, waits for them, and re-layouts  23.7 us
  transfers between devices with their start and end apart: 13, of which 11 were waited for; matrix products, arithmetic and copies ran while one was open for 19% of the time, Pallas kernels for 0%

profile of v1, /device:TPU:0, one launch (start us, length us, event | category | flops | bytes accessed | tf_op | source)
XLA Modules:
  0.0 793.2 jit_solution(703122421121879821)
XLA Ops:
  9.4 2.2 pad_maximum_fusion.6
  14.5 81.8 %all-gather.16.cloned.1.call-done = bf16[3840,640]{1,0:T(8,128)(2,1)} async-done(((bf16[480,640]{1,0:T(8,128)(2,1)}), bf16[3840,640]{1,0:T(8,128)(2,1)}) %all-gather.16.cloned.1.call-update) | async-done | bytes 4915216 | tf_op jit(solution)/shard_map/all_gather | solution.py:81
  96.3 2.8 fusion.62
  104.5 10.1 %all_gather.40 = bf16[512,960]{0,1:T(8,128)(2,1)} all-gather(bf16[128,960]{0,1:T(8,128)(2,1)S(1)} %copy-done.18), channel_id=1, replica_groups=mesh['dp'=4,'gx'=2,'gy'=4] {'dp'}, dimensions={0}, use_global_device_ids=true | all-gather | bytes 1228800 | tf_op jit(solution)/shard_map/all_gather | solution.py:260
  114.6 24.4 %all-gather.12.cloned.1.call-done = bf16[8,320,240]{2,1,0:T(8,128)(2,1)} async-done(((bf16[1,320,240]{2,1,0:T(8,128)(2,1)}), bf16[8,320,240]{2,1,0:T(8,128)(2,1)}) %all-gather.12.cloned.1.call-update) | async-done | bytes 1228816 | tf_op jit(solution)/shard_map/all_gather | solution.py:81
  139.0 2.3 copy.179
  141.3 2.1 reshape.312
  143.4 51.5 %all-gather.18.cloned.1.call-done = bf16[2560,480]{1,0:T(8,128)(2,1)} async-done(((bf16[320,480]{1,0:T(8,128)(2,1)}), bf16[2560,480]{1,0:T(8,128)(2,1)}) %all-gather.18.cloned.1.call-update) | async-done | bytes 2457616 | tf_op jit(solution)/shard_map/all_gather | solution.py:81
  194.9 5.9 copy.137
  200.8 5.7 reshape.309
  206.6 4.5 fusion.61
  211.0 2.8 copy.132
  213.8 3.9 reshape.299
  219.3 2.9 copy.134
  222.2 5.0 reshape.303
  227.3 10.2 %all-gather.10.cloned.1.call-done = bf16[1024,640]{0,1:T(8,128)(2,1)} async-done(((bf16[128,640]{0,1:T(8,128)(2,1)}), bf16[1024,640]{0,1:T(8,128)(2,1)}) %all-gather.10.cloned.1.call-update) | async-done | bytes 1310736 | tf_op jit(solution)/shard_map/all_gather | solution.py:248
  240.3 1.6 exponential_reduce_fusion
  241.9 1.5 copy-done
  243.4 2.0 convolution_convert_fusion.12
  246.6 9.7 %all_gather.36 = bf16[512,960]{0,1:T(8,128)(2,1)S(1)} all-gather(bf16[128,960]{0,1:T(8,128)(2,1)S(1)} %multiply_convert_fusion), channel_id=1, replica_groups=mesh['dp'=4,'gx'=2,'gy'=4] {'dp'}, dimensions={0}, use_global_device_ids=true | all-gather | bytes 1228800 | tf_op jit(solution)/shard_map/all_gather | solution.py:261
  256.3 1.6 convolution_convert_fusion.1
  260.8 2.4 convolution_convert_fusion.5
  263.2 2.3 copy.172
  265.9 3.7 convolution_convert_fusion.6
  269.6 2.3 copy.170
  272.0 15.9 %reduce-scatter.24.cloned.1.call-done = bf16[128,960]{1,0:T(8,128)(2,1)} async-done(((bf16[512,960]{1,0:T(8,128)(2,1)}), bf16[128,960]{1,0:T(8,128)(2,1)}) %reduce-scatter.24.cloned.1.call-update) | async-done | bytes 245776
  289.5 26.3 %reduce-scatter.22.cloned.1.call-done = bf16[128,960]{1,0:T(8,128)(2,1)} async-done(((bf16[512,960]{1,0:T(8,128)(2,1)}), bf16[128,960]{1,0:T(8,128)(2,1)}) %reduce-scatter.22.cloned.1.call-update) | async-done | bytes 245776
  315.7 1.8 copy.171
  317.5 2.3 fusion.29
  319.8 2.3 convolution_convert_fusion.9
  322.2 5.4 fusion.6
  327.6 2.8 fusion.1
  333.4 2.5 copy.174
  336.0 2.0 convolution_convert_fusion.3
  338.0 6.0 reshape.317
  344.0 3.2 copy.144
  347.4 3.1 convolution_multiply_fusion
  350.6 2.1 convolution_convert_fusion.2
  352.7 6.1 reshape.319
  358.7 3.1 copy.145
  361.9 39.2 %reduce-scatter.26.cloned.1.call-done = bf16[128,640]{1,0:T(8,128)(2,1)} async-done(((bf16[1024,640]{1,0:T(8,128)(2,1)}), bf16[128,640]{1,0:T(8,128)(2,1)}) %reduce-scatter.26.cloned.1.call-update) | async-done | bytes 163856
  403.5 3.5 reshape.321
  407.0 3.5 copy.146
  412.0 3.5 reshape.323
  415.5 3.6 copy.147
  419.0 3.7 pad_maximum_fusion.1
  423.0 4.5 convolution_convert_fusion
  427.5 4.4 copy.148
  431.9 5.8 reshape.325
  437.8 3.9 copy.149
  441.7 2.1 convolution_convert_fusion.4
  443.8 4.4 reshape.350
  448.1 5.1 copy.169
  453.3 1.6 copy.151
  455.4 3.1 pad_maximum_fusion
  458.5 12.5 %reduce-scatter.14.cloned.1.call-done = bf16[1,480,240]{2,1,0:T(8,128)(2,1)} async-done(((bf16[8,480,240]{2,1,0:T(8,128)(2,1)}), bf16[1,480,240]{2,1,0:T(8,128)(2,1)}) %reduce-scatter.14.cloned.1.call-update) | async-done | bytes 230416 | tf_op jit(solution)/shard_map/reduce_scatter | solution.py:101
  471.0 70.0 %reduce-scatter.16.cloned.1.call-done = bf16[1,480,240]{2,1,0:T(8,128)(2,1)} async-done(((bf16[8,480,240]{2,1,0:T(8,128)(2,1)}), bf16[1,480,240]{2,1,0:T(8,128)(2,1)}) %reduce-scatter.16.cloned.1.call-update) | async-done | bytes 230416 | tf_op jit(solution)/shard_map/reduce_scatter | solution.py:101
  541.0 69.7 %reduce-scatter.18.cloned.1.call-done = bf16[1,480,160]{2,1,0:T(8,128)(2,1)} async-done(((bf16[8,480,160]{2,1,0:T(8,128)(2,1)}), bf16[1,480,160]{2,1,0:T(8,128)(2,1)}) %reduce-scatter.18.cloned.1.call-update) | async-done | bytes 153616 | tf_op jit(solution)/shard_map/reduce_scatter | solution.py:101
  610.7 2.3 pad_maximum_fusion.7
  613.0 85.0 %reduce-scatter.20.cloned.1.call-done = bf16[1,320,720]{2,1,0:T(8,128)(2,1)} async-done(((bf16[8,320,720]{2,1,0:T(8,128)(2,1)}), bf16[1,320,720]{2,1,0:T(8,128)(2,1)}) %reduce-scatter.20.cloned.1.call-update) | async-done | bytes 460816 | tf_op jit(solution)/shard_map/reduce_scatter | solution.py:101
  698.0 1.5 fusion.68
  699.5 1.6 fusion.41
  702.6 69.5 %all-gather.3 = f32[32,2,960]{2,1,0:T(2,128)S(1)} all-gather(f32[1,2,960]{2,1,0:T(2,128)S(1)} %maximum_bitcast_fusion), channel_id=4, replica_groups=mesh['dp'=4,'gx'=2,'gy'=4] {'dp','gx','gy'}, dimensions={0}, use_global_device_ids=true | all-gather | bytes 253440 | tf_op jit(solution)/shard_map/all_gather | solution.py:345
  772.9 1.9 fusion.36
  (172 shorter events, 42.6 us)
Async XLA Ops:
  7.2 4.5 copy-start.24
  7.2 89.1 %all-gather.16.cloned.1.call-start = ((), (), s32[]{:S(2)}) async-start(), calls=%async_computation.15 | async-start | bytes 5529600 | tf_op jit(solution)/shard_map/all_gather | solution.py:81
  8.3 4.4 copy-start.25
  11.6 1.4 copy-start.26
  11.7 127.3 %all-gather.12.cloned.1.call-start = ((), (), s32[]{:S(2)}) async-start(), calls=%async_computation.8 | async-start | bytes 1474560 | tf_op jit(solution)/shard_map/all_gather | solution.py:81
  12.7 1.5 copy-start.3
  12.7 182.2 %all-gather.18.cloned.1.call-start = ((), (), s32[]{:S(2)}) async-start(), calls=%async_computation.16 | async-start | bytes 2949120 | tf_op jit(solution)/shard_map/all_gather | solution.py:81
  14.1 223.4 %all-gather.10.cloned.1.call-start = ((), (), s32[]{:S(2)}) async-start(), calls=%async_computation.7 | async-start | bytes 1474560 | tf_op jit(solution)/shard_map/all_gather | solution.py:248
  99.2 1.4 copy-start.28
  100.6 0.9 copy-start.9
  102.2 1.9 copy-start.30
  102.2 2.2 copy-start.18
  102.9 36.1 %copy-start.10 = (bf16[960,320]{0,1:T(8,128)(2,1)}, bf16[960,320]{0,1:T(8,128)(2,1)S(1)}, u32[]{:S(2)}) copy-start(bf16[960,320]{0,1:T(8,128)(2,1)S(1)} %reshape.295) | copy-start | bytes 1843204
  104.1 183.9 %reduce-scatter.24.cloned.1.call-start = ((), (), s32[]{:S(2)}) async-start(), calls=%async_computation.18 | async-start | bytes 1310720
  104.4 137.5 %copy-start.16 = (pred[128,1024]{0,1:T(8,128)(4,1)}, pred[128,1024]{0,1:T(8,128)(4,1)S(1)}, u32[]{:S(2)}) copy-start(pred[128,1024]{0,1:T(8,128)(4,1)S(1)} %fusion.26) | copy-start | bytes 393220
  217.7 1.5 copy-start.5
  238.9 1.4 copy-start.6
  238.9 3.0 copy-start.22
  240.3 3.1 copy-start
  243.4 2.0 copy-start.2
  245.4 10.8 %copy-start.12 = (bf16[5,64,3,128]{3,1,2,0:T(8,128)(2,1)}, bf16[5,64,3,128]{3,1,2,0:T(8,128)(2,1)S(1)}, u32[]{:S(2)}) copy-start(bf16[5,64,3,128]{3,1,2,0:T(8,128)(2,1)S(1)} %convolution_convert_fusion.12) | copy-start | bytes 737284
  245.4 1.0 copy-start.29
  245.4 10.8 %copy-start.8 = (bf16[1280,960]{1,0:T(8,128)(2,1)S(1)}, bf16[1280,960]{1,0:T(8,128)(2,1)}, u32[]{:S(2)}) copy-start(bf16[1280,960]{1,0:T(8,128)(2,1)} %reshape.309) | copy-start | bytes 7372804
  256.2 1.6 copy-start.21
  256.2 1.7 copy-start.15
  256.2 1.9 copy-start.19
  258.2 1.4 copy-start.33
  259.6 0.9 copy-start.31
  259.6 1.1 copy-start.32
  265.5 50.3 %reduce-scatter.22.cloned.1.call-start = ((), (), s32[]{:S(2)}) async-start(), calls=%async_computation.17 | async-start | bytes 1310720
  271.9 129.2 %reduce-scatter.26.cloned.1.call-start = ((), (), s32[]{:S(2)}) async-start(), calls=%async_computation.19 | async-start | bytes 1474560
  289.1 26.7 %copy-start.11 = (bf16[128,960]{0,1:T(8,128)(2,1)}, bf16[128,960]{0,1:T(8,128)(2,1)S(1)}, u32[]{:S(2)}) copy-start(bf16[128,960]{0,1:T(8,128)(2,1)S(1)} %copy.173) | copy-start | bytes 737284
  317.5 4.5 copy-start.13
  317.5 10.0 %slice-start = ((s8[7864320]{0:T(1024)(128)(4,1)}), s8[4194304]{0:T(1024)(128)(4,1)S(1)}, s32[]{:S(2)}) async-start(s8[7864320]{0:T(1024)(128)(4,1)} %bitcast.180), calls=%async_computation.20 | async-start | bytes 8388608
  319.8 2.4 copy-start.17
  322.2 5.4 slice-start.1
  322.2 5.4 copy-start.23
  330.4 1.9 copy-start.1
  333.4 2.5 copy-start.14
  335.9 135.1 %reduce-scatter.14.cloned.1.call-start = ((), (), s32[]{:S(2)}) async-start(), calls=%async_computation.9 | async-start | bytes 2211840 | tf_op jit(solution)/shard_map/reduce_scatter | solution.py:101
  347.2 193.8 %reduce-scatter.16.cloned.1.call-start = ((), (), s32[]{:S(2)}) async-start(), calls=%async_computation.10 | async-start | bytes 2211840 | tf_op jit(solution)/shard_map/reduce_scatter | solution.py:101
  361.9 248.8 %reduce-scatter.18.cloned.1.call-start = ((), (), s32[]{:S(2)}) async-start(), calls=%async_computation.11 | async-start | bytes 2211840 | tf_op jit(solution)/shard_map/reduce_scatter | solution.py:101
  402.2 8.3 %copy-start.27 = (bf16[128,640]{1,0:T(8,128)(2,1)S(1)}, bf16[128,640]{1,0:T(8,128)(2,1)}, u32[]{:S(2)}) copy-start(bf16[128,640]{1,0:T(8,128)(2,1)} %reduce-scatter.26.cloned.1.call-done) | copy-start | bytes 491524
  422.8 275.2 %reduce-scatter.20.cloned.1.call-start = ((), (), s32[]{:S(2)}) async-start(), calls=%async_computation.13 | async-start | bytes 4423680 | tf_op jit(solution)/shard_map/reduce_scatter | solution.py:101
  437.8 3.9 copy-start.20
  437.8 3.9 copy-start.34
  453.3 2.1 copy-start.4
  458.5 316.3 %all-reduce.2.cloned.1.call-start = ((), (), s32[]{:S(2)}) async-start(), calls=%async_computation.12 | async-start | bytes 1228800 | tf_op jit(solution)/shard_map/psum | solution.py:349
  613.0 165.7 %all-gather.14.cloned.1.call-start = ((), (), s32[]{:S(2)}) async-start(), calls=%async_computation.14 | async-start | bytes 2457600 | tf_op jit(solution)/shard_map/all_gather | solution.py:297
  774.8 2.8 copy-start.7
Sparse Core Ops, SparseCore 0:
  11.8 84.5 all-gather.15
  99.0 39.9 all-gather.11
  141.6 53.2 all-gather.17
  197.3 40.1 all-gather.9
  265.6 22.3 reduce-scatter.23
  290.9 24.8 reduce-scatter.21
  336.1 65.0 reduce-scatter.25
  404.6 66.3 reduce-scatter.13
  474.5 66.4 reduce-scatter.15
  544.3 66.2 reduce-scatter.17
  614.4 83.5 reduce-scatter.19
  700.8 33.4 all-reduce.1
  735.8 22.0 all-gather.13

commit v2 on v1

--- a/solution.py
+++ b/solution.py
@@ -99,6 +99,21 @@
 
 def scatter_blocks(blocks):
     return lax.psum_scatter(blocks, ("gx", "gy"), scatter_dimension=0, tiled=False)
+
+
+def exchange_sum(blocks, axes):
+    moved = lax.all_to_all(blocks, axes, split_axis=0, concat_axis=0, tiled=True)
+    return jnp.sum(moved.astype(jnp.float32), axis=0)
+
+
+def feature_share(rows):
+    fanin = lax.axis_size("gx")
+    replicas = lax.axis_size("dp")
+    count_of_rows, width = rows.shape
+    shaped = rows.reshape(count_of_rows, fanin, replicas, width // fanin // replicas)
+    shaped = shaped.transpose(2, 0, 1, 3).reshape(replicas, count_of_rows, -1)
+    moved = lax.all_to_all(shaped, "dp", split_axis=0, concat_axis=0, tiled=True)
+    return moved.reshape(replicas * count_of_rows, -1)
 
 
 def hidden_slice(weight, groups):
@@ -227,9 +242,14 @@
     up_part = hidden_slice(up_weight.T, 1)
     down_part = hidden_slice(down_weight, groups)
     share = gate_part.shape[0]
-    gate_up_blocks = gather_blocks(jnp.concatenate([gate_part, up_part], axis=0))
-    down_blocks = gather_blocks(down_part)
     model_block = gate_part.shape[1]
+    gate_up_part = jnp.concatenate([gate_part, up_part], axis=0)
+    if gate_up_part.shape[0] == down_part.shape[0]:
+        mlp_blocks = gather_blocks(jnp.concatenate([gate_up_part, down_part], axis=1))
+        gate_up_blocks, down_blocks = mlp_blocks[:, :, :model_block], mlp_blocks[:, :, model_block:]
+    else:
+        gate_up_blocks = gather_blocks(gate_up_part)
+        down_blocks = gather_blocks(down_part)
     gate_up_rows = (
         gate_up_blocks.reshape(fanin, fanout, 2, share, model_block)
         .transpose(2, 1, 3, 0, 4)
@@ -270,19 +290,19 @@
     ).astype(jnp.bfloat16)
     up_delta = (dactivated * gate_float * sigmoid_gate).astype(jnp.bfloat16)
     deltas = jnp.concatenate([gate_delta, up_delta], axis=1)
-    dnormed_two = lax.psum_scatter(
-        jnp.dot(deltas, gate_up_rows, preferred_element_type=jnp.float32).astype(jnp.bfloat16),
+    dnormed_two = exchange_sum(
+        jnp.dot(deltas, gate_up_rows, preferred_element_type=jnp.float32)
+        .astype(jnp.bfloat16)
+        .reshape(replicas, count_of_rows, -1),
         "dp",
-        scatter_dimension=0,
-        tiled=True,
-    ).astype(jnp.float32)
-    mlp_out = lax.psum_scatter(
-        jnp.dot(activated, down_rows, preferred_element_type=jnp.float32).astype(jnp.bfloat16),
+    )
+    mlp_out = exchange_sum(
+        jnp.dot(activated, down_rows, preferred_element_type=jnp.float32)
+        .astype(jnp.bfloat16)
+        .reshape(replicas, count_of_rows, -1),
         "dp",
-        scatter_dimension=0,
-        tiled=True,
-    )
-    layer_out = (hidden + mlp_out.astype(jnp.float32)).astype(jnp.bfloat16)
+    )
+    layer_out = (hidden + mlp_out).astype(jnp.bfloat16)
 
     gate_up_grad = (
         weight_product(deltas, normed_all)
@@ -311,29 +331,40 @@
     dhidden_norm, mlpgain_part = normalize_back(dnormed_two, mlp_gain, rms_two, unit_two)
     dhidden = cotangent.astype(jnp.float32) + dhidden_norm
     dhidden_bf = dhidden.astype(jnp.bfloat16)
-    output_sum = scatter_blocks(cut_blocks(weight_product(attention_mixture, dhidden_bf)))
+    hidden_all = lax.all_gather(dhidden_bf, "dp", axis=0, tiled=True)
+    output_blocks = cut_blocks(weight_product(feature_share(attention_mixture), hidden_all))
     mixture_gradient = back_product(dhidden_bf, output_full).astype(jnp.bfloat16)
     dquery_rot, dkey_seq, dvalue_seq = attend_back(
         rotated_query, key_all, value_all, allowed, logsum, attention_mixture, mixture_gradient
     )
-    dkv = lax.psum_scatter(
-        jnp.concatenate([dkey_seq, dvalue_seq], axis=1).astype(jnp.bfloat16),
+    dkv = exchange_sum(
+        jnp.concatenate([dkey_seq, dvalue_seq], axis=1)
+        .astype(jnp.bfloat16)
+        .reshape(fanin * fanout, count_of_rows, -1),
         ("gx", "gy"),
-        scatter_dimension=0,
-        tiled=True,
     )
     dquery = unrotate(dquery_rot, cos_table, sin_table).astype(jnp.bfloat16)
-    query_sum = scatter_blocks(cut_blocks(weight_product(normed_one, dquery)))
-    dkey = unrotate(dkv[:, :kv_width].astype(jnp.float32), cos_table, sin_table).astype(jnp.bfloat16)
-    dvalue_bf = dkv[:, kv_width:]
-    kv_sum = scatter_blocks(
+    dkey = unrotate(dkv[:, :kv_width], cos_table, sin_table).astype(jnp.bfloat16)
+    dvalue_bf = dkv[:, kv_width:].astype(jnp.bfloat16)
+    dattn_all = lax.all_gather(
+        jnp.concatenate([dquery, dkey, dvalue_bf], axis=1), "dp", axis=0, tiled=True
+    )
+    dattn_grad = weight_product(feature_share(normed_one), dattn_all)
+    query_columns = dquery.shape[1]
+    attn_sum = exchange_sum(
         jnp.concatenate(
             [
-                cut_blocks(weight_product(normed_one, dkey)),
-                cut_blocks(weight_product(normed_one, dvalue_bf)),
+                cut_blocks(dattn_grad[:, :query_columns]),
+                cut_blocks(dattn_grad[:, query_columns : query_columns + kv_width]),
+                cut_blocks(dattn_grad[:, query_columns + kv_width :]),
+                output_blocks,
             ],
             axis=2,
-        )
+        ),
+        ("gx", "gy"),
+    )
+    attn_sum = lax.all_gather(attn_sum.astype(jnp.bfloat16), "dp", axis=0, tiled=True).astype(
+        jnp.float32
     )
     dnormed_one = (
         back_product(dquery, query_full)
@@ -346,14 +377,10 @@
         jnp.stack([attgain_part, mlpgain_part]), ("dp", "gx", "gy"), axis=0, tiled=False
     )
     attgain_grad, mlpgain_grad = jnp.sum(gain_parts, axis=0)
-    attn_sum = lax.psum(jnp.concatenate([output_sum, query_sum, kv_sum], axis=1), "dp").astype(
-        jnp.float32
-    )
-    o_width = output_weight.shape[1]
-    output_grad = attn_sum[:, :o_width]
-    query_grad = attn_sum[:, o_width : o_width + q_width]
-    key_grad = attn_sum[:, o_width + q_width : o_width + q_width + k_width]
-    value_grad = attn_sum[:, o_width + q_width + k_width :]
+    query_grad = attn_sum[:, :q_width]
+    key_grad = attn_sum[:, q_width : q_width + k_width]
+    value_grad = attn_sum[:, q_width + k_width : q_width + k_width + v_width]
+    output_grad = attn_sum[:, q_width + k_width + v_width :]
     return (
         layer_out,
         input_grad,

time: 800 us -> 547 us (0.68)
  waiting for transfers between devices: 487 us -> 210 us
  blocking collectives: 89.3 us -> 123 us
  local copies, waits for them, and re-layouts: 131 us -> 109 us
  starting transfers between devices: 1.33 us -> 21.4 us
  matrix products: 48.1 us -> 38 us
    reduce_scatter x4 -> x1, waiting for transfers between devices: 237 us -> 41.1 us  [scatter_blocks(): lax.psum_scatter(blocks, ('gx', 'gy'), scatter_dimension=0, tiled=False)]
    unnamed x16 -> x6, waiting for transfers between devices: 81.6 us -> 0.1 us
    all_to_all x0 -> x5, waiting for transfers between devices: none -> 29.8 us  [the longest x3 28.6 us: exchange_sum(): lax.all_to_all(blocks, axes, split_axis=0, concat_axis=0, tiled=True)]
    all_gather x3 -> x2, waiting for transfers between devices: 158 us -> 130 us  [gather_blocks(): return lax.all_gather(block, ('gx', 'gy'), axis=0, tiled=False)]
    all_to_all x0 -> x5, starting transfers between devices: none -> 20.8 us  [the longest x3 12.8 us: exchange_sum(): lax.all_to_all(blocks, axes, split_axis=0, concat_axis=0, tiled=True)]
    all_gather x0 -> x2, blocking collectives: none -> 19.4 us  [the longest x1 12.4 us: on_device(): hidden_all = lax.all_gather(dhidden_bf, 'dp', axis=0, tiled=True)]
    all_to_all x0 -> x1, blocking collectives: none -> 16.5 us  [exchange_sum(): lax.all_to_all(blocks, axes, split_axis=0, concat_axis=0, tiled=True)]
    transpose x5 -> x1, local copies, waits for them, and re-layouts: 15 us -> 1.64 us  [cut_blocks(): grad.astype(jnp.bfloat16).reshape(fanin, rows, fanout, columns)]
  transfers between devices with their start and end apart: 13 -> 11, of which waited for: 11 -> 6; matrix products, arithmetic and copies ran while one was open for 19% -> 24% of each run, Pallas kernels for 0% -> 0%
where the time goes in v2:
time: 547 us; the launch traced here: 540 us
  waiting for transfers between devices  210 us (38%)
  blocking collectives  123 us (22%)
  local copies, waits for them, and re-layouts  109 us (20%)
  matrix products  38 us (7%)
  other arithmetic  24.1 us (4%)
  starting transfers between devices  21.4 us (4%)
  between operations  15.7 us (3%)
    all_gather x2, waiting for transfers between devices, gather_blocks(): return lax.all_gather(block, ('gx', 'gy'), axis=0, tiled=False)  130 us
    all_gather x1, blocking collectives, on_device(): lax.all_gather(jnp.stack([attgain_part, mlpgain_part]), ('dp', 'gx', 'gy'...  66.4 us
    reduce_scatter x1, waiting for transfers between devices, scatter_blocks(): lax.psum_scatter(blocks, ('gx', 'gy'), scatter_dimension=0, tiled=False)  41.1 us
    all_to_all x3, waiting for transfers between devices, exchange_sum(): lax.all_to_all(blocks, axes, split_axis=0, concat_axis=0, tiled=True)  28.6 us
    reshape x8, local copies, waits for them, and re-layouts, cut_blocks(): grad.astype(jnp.bfloat16).reshape(fanin, rows, fanout, columns)  20.4 us
    all_to_all x1, blocking collectives, exchange_sum(): lax.all_to_all(blocks, axes, split_axis=0, concat_axis=0, tiled=True)  16.5 us
    unnamed x102, local copies, waits for them, and re-layouts  13.9 us
    all_to_all x3, starting transfers between devices, exchange_sum(): lax.all_to_all(blocks, axes, split_axis=0, concat_axis=0, tiled=True)  12.8 us
  transfers between devices with their start and end apart: 11, of which 6 were waited for; matrix products, arithmetic and copies ran while one was open for 24% of the time, Pallas kernels for 0%

profile of v2, /device:TPU:0, one launch (start us, length us, event | category | flops | bytes accessed | tf_op | source)
XLA Modules:
  0.0 540.4 jit_solution(15195763862486439651)
XLA Ops:
  9.4 2.2 pad_maximum_fusion.6
  15.2 81.1 %all-gather.16.cloned.1.call-done = bf16[3840,640]{1,0:T(8,128)(2,1)} async-done(((bf16[480,640]{1,0:T(8,128)(2,1)}), bf16[3840,640]{1,0:T(8,128)(2,1)}) %all-gather.16.cloned.1.call-update) | async-done | bytes 4915216 | tf_op jit(solution)/shard_map/all_gather | solution.py:81
  96.3 2.9 fusion.52
  99.2 1.9 copy.147
  101.0 2.6 reshape.317
  106.8 10.6 %all_gather.45 = bf16[512,960]{0,1:T(8,128)(2,1)} all-gather(bf16[128,960]{0,1:T(8,128)(2,1)S(1)} %copy-done.10), channel_id=1, replica_groups=mesh['dp'=4,'gx'=2,'gy'=4] {'dp'}, dimensions={0}, use_global_device_ids=true | all-gather | bytes 1228800 | tf_op jit(solution)/shard_map/all_gather | solution.py:280
  117.5 49.3 %all-gather.18.cloned.1.call-done = bf16[2560,720]{1,0:T(8,128)(2,1)} async-done(((bf16[320,720]{1,0:T(8,128)(2,1)}), bf16[2560,720]{1,0:T(8,128)(2,1)}) %all-gather.18.cloned.1.call-update) | async-done | bytes 3686416 | tf_op jit(solution)/shard_map/all_gather | solution.py:81
  166.8 3.2 slice.140
  170.0 2.0 slice.137
  172.1 2.7 copy.156
  174.8 3.8 reshape.337
  178.6 2.3 copy.157
  180.9 2.0 reshape.339
  182.9 4.6 fusion.51
  187.5 1.5 copy.152
  189.0 2.8 reshape.329
  191.8 4.3 copy.150
  196.1 4.1 reshape.325
  201.3 8.3 %all-gather.10.cloned.1.call-done = bf16[1024,640]{0,1:T(8,128)(2,1)} async-done(((bf16[128,640]{0,1:T(8,128)(2,1)}), bf16[1024,640]{0,1:T(8,128)(2,1)}) %all-gather.10.cloned.1.call-update) | async-done | bytes 1310736 | tf_op jit(solution)/shard_map/all_gather | solution.py:268
  212.4 1.6 exponential_reduce_fusion
  214.0 2.0 convolution_convert_fusion.10
  217.2 9.7 %all_gather.42 = bf16[512,960]{0,1:T(8,128)(2,1)S(1)} all-gather(bf16[128,960]{0,1:T(8,128)(2,1)S(1)} %multiply_convert_fusion), channel_id=1, replica_groups=mesh['dp'=4,'gx'=2,'gy'=4] {'dp'}, dimensions={0}, use_global_device_ids=true | all-gather | bytes 1228800 | tf_op jit(solution)/shard_map/all_gather | solution.py:281
  226.8 1.6 convolution_convert_fusion.1
  230.2 1.5 fusion.8
  231.9 16.5 %all_to_all.30 = bf16[4,128,960]{1,2,0:T(8,128)(2,1)S(1)} all-to-all(bf16[4,128,960]{1,2,0:T(8,128)(2,1)S(1)} %bitcast.236), channel_id=1, replica_groups=mesh['dp'=4,'gx'=2,'gy'=4] {'dp'}, dimensions={0} | all-to-all | bytes 1966080 | tf_op jit(solution)/shard_map/all_to_all | solution.py:105
  250.0 2.1 fusion.6
  252.1 2.8 fusion.1
  258.3 4.3 all-to-all-start.2
  262.7 3.1 convolution_multiply_fusion
  266.5 28.5 %all-to-all-done.2 = bf16[8,128,640]{1,2,0:T(8,128)(2,1)} async-done(((bf16[8,128,640]{1,2,0:T(8,128)(2,1)}), bf16[8,128,640]{1,2,0:T(8,128)(2,1)}, u32[]{:S(2)}, u32[]{:S(2)}) %all-to-all-start.2) | async-done | bytes 1310752 | tf_op jit(solution)/shard_map/all_to_all | solution.py:105
  295.1 1.6 convert_reduce_fusion
  298.9 4.5 convolution_convert_fusion
  303.5 4.7 copy.178
  308.2 5.8 %reshape.357 = bf16[2,4,160,2,480]{4,3,2,1,0:T(2,128)(2,1)} reshape(bf16[1280,960]{1,0:T(8,128)(2,1)} %copy.178) | data formatting | bytes 4915200 | tf_op jit(solution)/shard_map/reshape | solution.py:310
  314.0 4.0 copy.179
  318.0 2.1 convolution_convert_fusion.3
  320.1 4.4 reshape.379
  324.5 5.1 copy.201
  329.6 1.6 copy.181
  331.7 3.0 pad_maximum_fusion
  335.5 4.0 all-to-all-start.3
  339.5 2.8 fusion.7
  345.4 4.0 all-to-all-start.4
  349.4 12.4 %all_gather.47 = bf16[512,960]{0,1:T(8,128)(2,1)} all-gather(bf16[128,960]{0,1:T(8,128)(2,1)S(1)} %copy-done.14), channel_id=1, replica_groups=mesh['dp'=4,'gx'=2,'gy'=4] {'dp'}, dimensions={0}, use_global_device_ids=true | all-gather | bytes 1228800 | tf_op jit(solution)/shard_map/all_gather | solution.py:334
  361.8 4.2 all-to-all-start
  366.1 2.6 convolution_convert_fusion.6
  368.7 2.3 reshape.355
  371.0 1.9 copy.175
  372.9 2.3 convolution_convert_fusion.2
  376.9 2.3 reshape.347
  379.2 1.9 copy.168
  381.1 1.8 fusion.55
  384.9 1.7 copy.171
  386.6 1.7 reshape.351
  388.3 1.8 copy.200
  390.1 2.9 pad_maximum_fusion.3
  393.0 4.3 all-to-all-start.5
  397.6 41.1 %reduce-scatter.2.cloned.1.call-done = bf16[1,320,720]{2,1,0:T(8,128)(2,1)} async-done(((bf16[8,320,720]{2,1,0:T(8,128)(2,1)}), bf16[1,320,720]{2,1,0:T(8,128)(2,1)}) %reduce-scatter.2.cloned.1.call-update) | async-done | bytes 460816 | tf_op jit(solution)/shard_map/reduce_scatter | solution.py:101
  438.8 2.2 convert_reduce_fusion.2
  441.1 1.6 fusion.61
  444.6 66.4 %all-gather.3 = f32[32,2,960]{2,1,0:T(2,128)S(1)} all-gather(f32[1,2,960]{2,1,0:T(2,128)S(1)} %maximum_bitcast_fusion), channel_id=4, replica_groups=mesh['dp'=4,'gx'=2,'gy'=4] {'dp','gx','gy'}, dimensions={0}, use_global_device_ids=true | all-gather | bytes 253440 | tf_op jit(solution)/shard_map/all_gather | solution.py:376
  511.8 2.2 fusion.32
  515.5 7.0 %all_gather.48 = bf16[480,640]{1,0:T(8,128)(2,1)S(1)} all-gather(bf16[120,640]{1,0:T(8,128)(2,1)S(1)} %reduce_sum.129), channel_id=1, replica_groups=mesh['dp'=4,'gx'=2,'gy'=4] {'dp'}, dimensions={0}, use_global_device_ids=true | all-gather | bytes 768000 | tf_op jit(solution)/shard_map/all_gather | solution.py:366
  525.2 1.5 slice.156
  (190 shorter events, 45.2 us)
Async XLA Ops:
  7.2 4.5 copy-start.30
  7.2 4.8 copy-start.31
  7.2 89.1 %all-gather.16.cloned.1.call-start = ((), (), s32[]{:S(2)}) async-start(), calls=%async_computation.11 | async-start | bytes 5529600 | tf_op jit(solution)/shard_map/all_gather | solution.py:81
  11.6 155.2 %all-gather.18.cloned.1.call-start = ((), (), s32[]{:S(2)}) async-start(), calls=%async_computation.12 | async-start | bytes 4423680 | tf_op jit(solution)/shard_map/all_gather | solution.py:81
  12.2 2.5 copy-start.4
  12.2 2.8 copy-start.33
  14.6 195.0 %all-gather.10.cloned.1.call-start = ((), (), s32[]{:S(2)}) async-start(), calls=%async_computation.7 | async-start | bytes 1474560 | tf_op jit(solution)/shard_map/all_gather | solution.py:268
  14.9 84.3 %copy-start.36 = (f32[128]{0:T(128)}, f32[128]{0:T(128)S(1)}, u32[]{:S(2)}) copy-start(f32[128]{0:T(128)S(1)} %add_rsqrt_fusion.1) | copy-start | bytes 1540
  103.6 1.8 copy-start.5
  104.4 2.1 copy-start.38
  105.0 12.5 %copy-start.6 = (bf16[960,320]{0,1:T(8,128)(2,1)}, bf16[960,320]{0,1:T(8,128)(2,1)S(1)}, u32[]{:S(2)}) copy-start(bf16[960,320]{0,1:T(8,128)(2,1)S(1)} %reshape.321) | copy-start | bytes 1843204
  105.0 1.8 copy-start.10
  106.8 107.2 %copy-start.24 = (pred[128,1024]{0,1:T(8,128)(4,1)}, pred[128,1024]{0,1:T(8,128)(4,1)S(1)}, u32[]{:S(2)}) copy-start(pred[128,1024]{0,1:T(8,128)(4,1)S(1)} %fusion.26) | copy-start | bytes 393220
  201.3 11.0 %copy-start.19 = (bf16[128,15,64]{0,2,1:T(8,128)(2,1)}, bf16[128,15,64]{0,2,1:T(8,128)(2,1)S(1)}, u32[]{:S(2)}) copy-start(bf16[128,15,64]{0,2,1:T(8,128)(2,1)S(1)} %pad_maximum_fusion.9) | copy-start | bytes 737284
  211.0 1.4 copy-start.3
  214.0 2.0 copy-start.1
  216.0 33.9 %copy-start.17 = (bf16[5,64,3,128]{3,1,2,0:T(8,128)(2,1)}, bf16[5,64,3,128]{3,1,2,0:T(8,128)(2,1)S(1)}, u32[]{:S(2)}) copy-start(bf16[5,64,3,128]{3,1,2,0:T(8,128)(2,1)S(1)} %convolution_convert_fusion.10) | copy-start | bytes 737284
  216.0 1.0 copy-start.32
  216.0 10.8 %copy-start.9 = (bf16[1280,960]{1,0:T(8,128)(2,1)S(1)}, bf16[1280,960]{1,0:T(8,128)(2,1)}, u32[]{:S(2)}) copy-start(bf16[1280,960]{1,0:T(8,128)(2,1)} %reshape.337) | copy-start | bytes 7372804
  216.9 32.0 %copy-start.34 = (f32[128]{0:T(128)}, f32[128]{0:T(128)S(1)}, u32[]{:S(2)}) copy-start(f32[128]{0:T(128)S(1)} %add_rsqrt_fusion) | copy-start | bytes 1540
  226.8 1.6 copy-start.28
  226.8 1.7 copy-start.23
  226.8 1.9 copy-start.26
  228.8 1.4 copy-start.43
  230.2 1.5 copy-start.41
  230.2 1.5 copy-start.42
  231.9 17.0 %copy-start.11 = (bf16[128,960]{0,1:T(8,128)(2,1)S(1)}, bf16[128,960]{0,1:T(8,128)(2,1)}, u32[]{:S(2)}) copy-start(bf16[128,960]{0,1:T(8,128)(2,1)} %param.23) | copy-start | bytes 737284
  248.9 0.9 copy-start.39
  248.9 1.0 copy-start.25
  249.2 0.7 copy-start.13
  252.0 2.8 copy-start.20
  254.8 1.9 copy-start
  258.3 36.7 %all-to-all-start.2 = ((bf16[8,128,640]{1,2,0:T(8,128)(2,1)}), bf16[8,128,640]{1,2,0:T(8,128)(2,1)}, u32[]{:S(2)}, u32[]{:S(2)}) async-start(bf16[8,128,640]{1,2,0:T(8,128)(2,1)} %pad_maximum_fusion.2), calls=%async_computation.2 | async-start | bytes 2621440 | tf_op jit(solution)/shard_map/all_to_all | solution.py:105
  262.6 110.2 %all-gather.12.cloned.1.call-start = ((), (), s32[]{:S(2)}) async-start(), calls=%async_computation.8 | async-start | bytes 2048000 | tf_op jit(solution)/shard_map/all_gather | solution.py:349
  295.1 3.0 copy-start.15
  296.6 0.7 copy-start.21
  297.4 0.6 copy-start.29
  298.9 139.9 %reduce-scatter.2.cloned.1.call-start = ((), (), s32[]{:S(2)}) async-start(), calls=%async_computation.9 | async-start | bytes 4423680 | tf_op jit(solution)/shard_map/reduce_scatter | solution.py:101
  314.0 4.0 copy-start.27
  314.0 4.0 copy-start.44
  329.6 2.1 copy-start.2
  335.5 9.9 %all-to-all-start.3 = ((bf16[4,128,240]{1,2,0:T(8,128)(2,1)}), bf16[4,128,240]{1,2,0:T(8,128)(2,1)}, u32[]{:S(2)}, u32[]{:S(2)}) async-start(bf16[4,128,240]{1,2,0:T(8,128)(2,1)} %bitcast.256), calls=%async_computation.3 | async-start | bytes 491520 | tf_op jit(solution)/shard_map/all_to_all | solution.py:115
  339.5 2.9 copy-start.18
  342.3 7.1 %copy-start.14 = (bf16[128,960]{0,1:T(8,128)(2,1)S(1)}, bf16[128,960]{0,1:T(8,128)(2,1)}, u32[]{:S(2)}) copy-start(bf16[128,960]{0,1:T(8,128)(2,1)} %copy-done.13) | copy-start | bytes 737284
  345.4 16.4 %all-to-all-start.4 = ((bf16[4,128,240]{1,2,0:T(8,128)(2,1)}), bf16[4,128,240]{1,2,0:T(8,128)(2,1)}, u32[]{:S(2)}, u32[]{:S(2)}) async-start(bf16[4,128,240]{1,2,0:T(8,128)(2,1)} %bitcast.255), calls=%async_computation.4 | async-start | bytes 491520 | tf_op jit(solution)/shard_map/all_to_all | solution.py:115
  361.8 31.2 %all-to-all-start = ((bf16[4,128,960]{1,2,0:T(8,128)(2,1)}), bf16[4,128,960]{1,2,0:T(8,128)(2,1)}, u32[]{:S(2)}, u32[]{:S(2)}) async-start(bf16[4,128,960]{1,2,0:T(8,128)(2,1)} %bitcast.235), calls=%async_computation | async-start | bytes 1966080 | tf_op jit(solution)/shard_map/all_to_all | solution.py:105
  375.2 0.9 copy-start.8
  393.0 121.0 %all-to-all-start.5 = ((bf16[8,120,640]{2,1,0:T(8,128)(2,1)}), bf16[8,120,640]{2,1,0:T(8,128)(2,1)}, u32[]{:S(2)}, u32[]{:S(2)}) async-start(bf16[8,120,640]{2,1,0:T(8,128)(2,1)} %pad_maximum_fusion.3), calls=%async_computation.5 | async-start | bytes 2457600 | tf_op jit(solution)/shard_map/all_to_all | solution.py:105
  397.3 45.4 %copy-start.22 = (f32[128,640]{0,1:T(8,128)S(1)}, f32[128,640]{0,1:T(8,128)}, u32[]{:S(2)}) copy-start(f32[128,640]{0,1:T(8,128)} %copy-done.21) | copy-start | bytes 983044
  397.3 127.9 %all-gather.14.cloned.1.call-start = ((), (), s32[]{:S(2)}) async-start(), calls=%async_computation.10 | async-start | bytes 2457600 | tf_op jit(solution)/shard_map/all_gather | solution.py:317
  438.8 3.9 copy-start.7
  438.8 4.3 copy-start.16
  438.8 4.3 copy-start.37
  443.1 68.6 %copy-start.12 = (bf16[128,960]{0,1:T(8,128)(2,1)S(1)}, bf16[128,960]{0,1:T(8,128)(2,1)}, u32[]{:S(2)}) copy-start(bf16[128,960]{0,1:T(8,128)(2,1)} %param.23) | copy-start | bytes 737284
  443.1 68.6 %copy-start.35 = (f32[128]{0:T(128)S(1)}, f32[128]{0:T(128)}, u32[]{:S(2)}) copy-start(f32[128]{0:T(128)} %copy-done.34) | copy-start | bytes 1540
  443.1 68.6 %copy-start.40 = (f32[128]{0:T(128)S(1)}, f32[128]{0:T(128)}, u32[]{:S(2)}) copy-start(f32[128]{0:T(128)} %copy-done.39) | copy-start | bytes 1540
Sparse Core Ops, SparseCore 0:
  11.7 84.5 all-gather.15
  99.0 67.7 all-gather.17
  169.4 40.1 all-gather.9
  299.0 16.5 all-gather.11
  334.9 103.8 reduce-scatter.1
  440.2 20.0 all-gather.13

commit v3 on v2

--- a/solution.py
+++ b/solution.py
@@ -312,6 +312,9 @@
         .reshape(fanin * fanout, 2 * share, model_block)
     )
     down_grad_blocks = cut_blocks(weight_product(activated, cot_all))
+    dnormed_two, gate_up_grad, down_grad_blocks = lax.optimization_barrier(
+        (dnormed_two, gate_up_grad, down_grad_blocks)
+    )
     if groups * share == 2 * share:
         mlp_sum = scatter_blocks(jnp.concatenate([gate_up_grad, down_grad_blocks], axis=2))
         mlp_sum = lax.all_gather(mlp_sum, "dp", axis=0, tiled=False)
@@ -331,8 +334,6 @@
     dhidden_norm, mlpgain_part = normalize_back(dnormed_two, mlp_gain, rms_two, unit_two)
     dhidden = cotangent.astype(jnp.float32) + dhidden_norm
     dhidden_bf = dhidden.astype(jnp.bfloat16)
-    hidden_all = lax.all_gather(dhidden_bf, "dp", axis=0, tiled=True)
-    output_blocks = cut_blocks(weight_product(feature_share(attention_mixture), hidden_all))
     mixture_gradient = back_product(dhidden_bf, output_full).astype(jnp.bfloat16)
     dquery_rot, dkey_seq, dvalue_seq = attend_back(
         rotated_query, key_all, value_all, allowed, logsum, attention_mixture, mixture_gradient
@@ -346,26 +347,12 @@
     dquery = unrotate(dquery_rot, cos_table, sin_table).astype(jnp.bfloat16)
     dkey = unrotate(dkv[:, :kv_width], cos_table, sin_table).astype(jnp.bfloat16)
     dvalue_bf = dkv[:, kv_width:].astype(jnp.bfloat16)
-    dattn_all = lax.all_gather(
-        jnp.concatenate([dquery, dkey, dvalue_bf], axis=1), "dp", axis=0, tiled=True
-    )
-    dattn_grad = weight_product(feature_share(normed_one), dattn_all)
-    query_columns = dquery.shape[1]
-    attn_sum = exchange_sum(
-        jnp.concatenate(
-            [
-                cut_blocks(dattn_grad[:, :query_columns]),
-                cut_blocks(dattn_grad[:, query_columns : query_columns + kv_width]),
-                cut_blocks(dattn_grad[:, query_columns + kv_width :]),
-                output_blocks,
-            ],
-            axis=2,
-        ),
-        ("gx", "gy"),
-    )
-    attn_sum = lax.all_gather(attn_sum.astype(jnp.bfloat16), "dp", axis=0, tiled=True).astype(
-        jnp.float32
-    )
+    grads_all = lax.all_gather(
+        jnp.concatenate([dquery, dkey, dvalue_bf, dhidden_bf], axis=1), "dp", axis=0, tiled=True
+    )
+    dattn_width = dquery.shape[1] + 2 * kv_width
+    dattn_all, hidden_all = grads_all[:, :dattn_width], grads_all[:, dattn_width:]
+    output_blocks = cut_blocks(weight_product(feature_share(attention_mixture), hidden_all))
     dnormed_one = (
         back_product(dquery, query_full)
         + back_product(dkey, key_full)
@@ -373,10 +360,35 @@
     )
     dresidual, attgain_part = normalize_back(dnormed_one, attn_gain, rms_one, unit_one)
     input_grad = (dhidden + dresidual).astype(jnp.bfloat16)
-    gain_parts = lax.all_gather(
-        jnp.stack([attgain_part, mlpgain_part]), ("dp", "gx", "gy"), axis=0, tiled=False
-    )
-    attgain_grad, mlpgain_grad = jnp.sum(gain_parts, axis=0)
+    gain_parts = jnp.concatenate([attgain_part, mlpgain_part]).astype(jnp.bfloat16)
+    packed_width = packed.shape[1]
+    gain_rows = -(-gain_parts.shape[0] // (8 * packed_width)) * 8
+    gain_parts = jnp.pad(gain_parts, (0, gain_rows * packed_width - gain_parts.shape[0]))
+    gain_parts = jnp.broadcast_to(
+        gain_parts.reshape(1, gain_rows, packed_width), (fanin * fanout, gain_rows, packed_width)
+    )
+    dattn_grad = weight_product(feature_share(normed_one), dattn_all)
+    query_columns = dquery.shape[1]
+    attn_blocks_grad = jnp.concatenate(
+        [
+            cut_blocks(dattn_grad[:, :query_columns]),
+            cut_blocks(dattn_grad[:, query_columns : query_columns + kv_width]),
+            cut_blocks(dattn_grad[:, query_columns + kv_width :]),
+            output_blocks,
+        ],
+        axis=2,
+    )
+    attn_sum = exchange_sum(
+        jnp.concatenate([attn_blocks_grad, gain_parts], axis=1), ("gx", "gy")
+    )
+    attn_sum = lax.all_gather(attn_sum.astype(jnp.bfloat16), "dp", axis=0, tiled=False).astype(
+        jnp.float32
+    )
+    share_rows = attn_blocks_grad.shape[1]
+    gains = jnp.sum(attn_sum[:, share_rows:], axis=0).reshape(-1)
+    width = attn_gain.shape[0]
+    attgain_grad, mlpgain_grad = gains[:width], gains[width : 2 * width]
+    attn_sum = attn_sum[:, :share_rows].reshape(replicas * share_rows, packed_width)
     query_grad = attn_sum[:, :q_width]
     key_grad = attn_sum[:, q_width : q_width + k_width]
     value_grad = attn_sum[:, q_width + k_width : q_width + k_width + v_width]

time: 547 us -> 509 us (0.931)
  blocking collectives: 123 us -> 28.6 us
  waiting for transfers between devices: 210 us -> 256 us
    all_gather x3 -> x1, blocking collectives: 85.8 us -> 8.31 us  [on_device(): lax.all_gather(attn_sum.astype(jnp.bfloat16), 'dp', axis=0, tiled=False)]
    reduce_scatter x1, waiting for transfers between devices: 41.1 us -> 78.2 us  [scatter_blocks(): lax.psum_scatter(blocks, ('gx', 'gy'), scatter_dimension=0, tiled=False)]
    all_to_all x1 -> x0, blocking collectives: 16.5 us -> none  [exchange_sum(): lax.all_to_all(blocks, axes, split_axis=0, concat_axis=0, tiled=True)]
    all_gather x1, waiting for transfers between devices: 0.01 us -> 7.29 us  [on_device(): mlp_sum = lax.all_gather(mlp_sum, 'dp', axis=0, tiled=False)]
    all_to_all x3 -> x4, starting transfers between devices: 12.8 us -> 15.8 us  [exchange_sum(): lax.all_to_all(blocks, axes, split_axis=0, concat_axis=0, tiled=True)]
    unnamed x102 -> x110, local copies, waits for them, and re-layouts: 13.9 us -> 15.4 us
    all_to_all x3 -> x4, waiting for transfers between devices: 28.6 us -> 29 us  [exchange_sum(): lax.all_to_all(blocks, axes, split_axis=0, concat_axis=0, tiled=True)]
  transfers between devices with their start and end apart: 11 -> 12, of which waited for: 6 -> 8; matrix products, arithmetic and copies ran while one was open for 24% -> 26% of each run, Pallas kernels for 0% -> 0%
where the time goes in v3:
time: 509 us; the launch traced here: 502 us
  waiting for transfers between devices  256 us (50%)
  local copies, waits for them, and re-layouts  108 us (21%)
  matrix products  42.6 us (8%)
  blocking collectives  28.6 us (6%)
  other arithmetic  27 us (5%)
  starting transfers between devices  24.4 us (5%)
  between operations  15.8 us (3%)
    all_gather x2, waiting for transfers between devices, gather_blocks(): return lax.all_gather(block, ('gx', 'gy'), axis=0, tiled=False)  130 us
    reduce_scatter x1, waiting for transfers between devices, scatter_blocks(): lax.psum_scatter(blocks, ('gx', 'gy'), scatter_dimension=0, tiled=False)  78.2 us
    all_to_all x4, waiting for transfers between devices, exchange_sum(): lax.all_to_all(blocks, axes, split_axis=0, concat_axis=0, tiled=True)  29 us
    all_to_all x4, starting transfers between devices, exchange_sum(): lax.all_to_all(blocks, axes, split_axis=0, concat_axis=0, tiled=True)  15.8 us
    unnamed x110, local copies, waits for them, and re-layouts  15.4 us
    reshape x8, local copies, waits for them, and re-layouts, cut_blocks(): grad.astype(jnp.bfloat16).reshape(fanin, rows, fanout, columns)  15 us
    reshape x5, local copies, waits for them, and re-layouts, whole_weight(): return shaped.reshape(fanin * rows, fanout * columns)  12 us
    transpose x5, local copies, waits for them, and re-layouts, whole_weight(): shaped = blocks.reshape(fanin, fanout, rows, columns).transpose(0, 2, 1, 3)  10.8 us
  transfers between devices with their start and end apart: 12, of which 8 were waited for; matrix products, arithmetic and copies ran while one was open for 26% of the time, Pallas kernels for 0%

profile of v3, /device:TPU:0, one launch (start us, length us, event | category | flops | bytes accessed | tf_op | source)
XLA Modules:
  0.0 502.2 jit_solution(8690209817745039194)
XLA Ops:
  9.4 2.2 pad_maximum_fusion.7
  15.2 81.1 %all-gather.15.cloned.1.call-done = bf16[3840,640]{1,0:T(8,128)(2,1)} async-done(((bf16[480,640]{1,0:T(8,128)(2,1)}), bf16[3840,640]{1,0:T(8,128)(2,1)}) %all-gather.15.cloned.1.call-update) | async-done | bytes 4915216 | tf_op jit(solution)/shard_map/all_gather | solution.py:81
  96.3 2.8 fusion.57
  99.1 1.9 copy.147
  101.0 2.6 reshape.325
  107.4 10.6 %all_gather.39 = bf16[512,960]{0,1:T(8,128)(2,1)} all-gather(bf16[128,960]{0,1:T(8,128)(2,1)S(1)} %copy-done.12), channel_id=1, replica_groups=mesh['dp'=4,'gx'=2,'gy'=4] {'dp'}, dimensions={0}, use_global_device_ids=true | all-gather | bytes 1228800 | tf_op jit(solution)/shard_map/all_gather | solution.py:280
  118.1 48.8 %all-gather.17.cloned.1.call-done = bf16[2560,720]{1,0:T(8,128)(2,1)} async-done(((bf16[320,720]{1,0:T(8,128)(2,1)}), bf16[2560,720]{1,0:T(8,128)(2,1)}) %all-gather.17.cloned.1.call-update) | async-done | bytes 3686416 | tf_op jit(solution)/shard_map/all_gather | solution.py:81
  166.8 3.2 slice.164
  170.1 2.0 slice.161
  172.1 2.7 copy.156
  174.8 3.8 reshape.345
  178.6 2.3 copy.157
  181.0 2.0 reshape.347
  182.9 4.6 fusion.56
  187.5 1.5 copy.152
  189.0 2.8 reshape.337
  191.8 4.4 copy.150
  196.2 4.1 reshape.333
  201.4 8.3 %all-gather.9.cloned.1.call-done = bf16[1024,640]{0,1:T(8,128)(2,1)} async-done(((bf16[128,640]{0,1:T(8,128)(2,1)}), bf16[1024,640]{0,1:T(8,128)(2,1)}) %all-gather.9.cloned.1.call-update) | async-done | bytes 1310736 | tf_op jit(solution)/shard_map/all_gather | solution.py:268
  212.4 1.6 exponential_reduce_fusion
  214.1 1.5 copy-done
  215.5 2.0 convolution_convert_fusion.10
  218.7 9.7 %all_gather.36 = bf16[512,960]{0,1:T(8,128)(2,1)S(1)} all-gather(bf16[128,960]{0,1:T(8,128)(2,1)S(1)} %multiply_convert_fusion), channel_id=1, replica_groups=mesh['dp'=4,'gx'=2,'gy'=4] {'dp'}, dimensions={0}, use_global_device_ids=true | all-gather | bytes 1228800 | tf_op jit(solution)/shard_map/all_gather | solution.py:281
  228.4 1.6 convolution_convert_fusion.1
  231.7 1.5 fusion.9
  234.4 4.5 all-to-all-start.1
  238.8 4.6 convolution_convert_fusion
  243.4 4.5 copy.161
  247.9 5.8 %reshape.350 = bf16[2,4,160,2,480]{4,3,2,1,0:T(2,128)(2,1)} reshape(bf16[1280,960]{1,0:T(8,128)(2,1)} %copy.161) | data formatting | bytes 4915200 | tf_op jit(solution)/shard_map/reshape | solution.py:310
  253.7 4.0 copy.162
  257.7 2.1 convolution_convert_fusion.3
  259.8 4.4 reshape.387
  264.2 5.2 %copy.199 = bf16[2,320,4,240]{3,2,1,0:T(4,128)(2,1)} copy(bf16[2,320,4,240]{1,0,3,2:T(2,128)(2,1)} %reshape.387) | data formatting | bytes 2457600 | tf_op jit(solution)/shard_map/reshape | solution.py:96
  269.3 2.6 copy.164
  271.9 1.5 convert_reduce_fusion.1
  276.0 5.4 %fusion.7 = bf16[5,64,1024]{2,1,0:T(8,128)(2,1)S(1)} fusion(bf16[128,5,3,64]{0,3,2,1:T(8,128)(2,1)S(1)} %bitcast.258, f32[5,1024,128,3]{2,1,3,0:T(8,128)} %copy-done, f32[5,3,128]{2,1,0:T(4,128)S(1)} %log_add_fusion, pred[128,1024]{0,1:T(8,128)(4,1)S(1)} %copy-done.26), kind=kOutput, calls=%fused_computation.30 | convolution fusion | flops 259850240 | bytes 8904192 | tf_op jit(solution)/shard_map/kgtu,tkgd->ukd/dot_general | solution.py:197
  281.4 2.8 fusion.1
  287.7 4.3 all-to-all-start.2
  292.3 3.1 convolution_multiply_fusion
  296.1 29.0 %all-to-all-done.2 = bf16[8,128,640]{1,2,0:T(8,128)(2,1)} async-done(((bf16[8,128,640]{1,2,0:T(8,128)(2,1)}), bf16[8,128,640]{1,2,0:T(8,128)(2,1)}, u32[]{:S(2)}, u32[]{:S(2)}) %all-to-all-start.2) | async-done | bytes 1310752 | tf_op jit(solution)/shard_map/all_to_all | solution.py:105
  325.1 1.6 convert_reduce_fusion
  328.5 5.1 %pad_maximum_fusion = bf16[8,320,720]{2,1,0:T(8,128)(2,1)} fusion(bf16[8,320,240]{2,1,0:T(8,128)(2,1)} %bitcast.232, bf16[8,320,480]{2,1,0:T(8,128)(2,1)} %bitcast.219), kind=kLoop, calls=%fused_computation.8 | loop fusion | flops 7372800 | bytes 7372800 | tf_op jit(solution)/shard_map/concatenate | solution.py:319
  334.4 4.0 all-to-all-start.3
  338.4 1.7 copy.177
  340.1 2.8 fusion.8
  347.3 4.0 all-to-all-start.4
  351.4 3.1 fusion.35
  355.3 2.0 all-to-all-done.4
  357.3 3.5 all-to-all-start
  360.8 1.8 convolution_convert_fusion.6
  363.2 2.2 convolution_convert_fusion.2
  368.8 1.8 fusion.62
  372.6 1.7 copy.175
  374.3 1.7 reshape.363
  376.0 1.8 copy.201
  378.5 2.6 pad_maximum_fusion.3
  382.1 3.6 all-to-all-start.5
  385.8 78.2 %reduce-scatter.2.cloned.1.call-done = bf16[1,320,720]{2,1,0:T(8,128)(2,1)} async-done(((bf16[8,320,720]{2,1,0:T(8,128)(2,1)}), bf16[1,320,720]{2,1,0:T(8,128)(2,1)}) %reduce-scatter.2.cloned.1.call-update) | async-done | bytes 460816 | tf_op jit(solution)/shard_map/reduce_scatter | solution.py:101
  465.5 2.1 fusion.34
  467.8 8.3 %all-gather.2 = bf16[512,640]{1,0:T(8,128)(2,1)S(1)} all-gather(bf16[128,640]{1,0:T(8,128)(2,1)S(1)} %reduce_sum.131), channel_id=4, replica_groups=mesh['dp'=4,'gx'=2,'gy'=4] {'dp'}, dimensions={0}, use_global_device_ids=true | all-gather | bytes 819200 | tf_op jit(solution)/shard_map/all_gather | solution.py:384
  479.8 7.3 %all-gather.13.cloned.1.call-done = bf16[4,320,720]{2,1,0:T(8,128)(2,1)} async-done(((bf16[1,320,720]{2,1,0:T(8,128)(2,1)}), bf16[4,320,720]{2,1,0:T(8,128)(2,1)}) %all-gather.13.cloned.1.call-update) | async-done | bytes 1843216 | tf_op jit(solution)/shard_map/all_gather | solution.py:320
  487.1 1.5 slice.183
  491.8 1.4 copy.186
  493.5 1.4 copy.185
  (203 shorter events, 48.2 us)
Async XLA Ops:
  7.2 4.5 copy-start.33
  7.2 4.8 copy-start.34
  7.2 89.1 %all-gather.15.cloned.1.call-start = ((), (), s32[]{:S(2)}) async-start(), calls=%async_computation.11 | async-start | bytes 5529600 | tf_op jit(solution)/shard_map/all_gather | solution.py:81
  11.6 155.2 %all-gather.17.cloned.1.call-start = ((), (), s32[]{:S(2)}) async-start(), calls=%async_computation.12 | async-start | bytes 4423680 | tf_op jit(solution)/shard_map/all_gather | solution.py:81
  12.2 2.5 copy-start.5
  12.2 2.8 copy-start.36
  14.6 195.1 %all-gather.9.cloned.1.call-start = ((), (), s32[]{:S(2)}) async-start(), calls=%async_computation.7 | async-start | bytes 1474560 | tf_op jit(solution)/shard_map/all_gather | solution.py:268
  14.9 336.5 %copy-start.37 = (f32[128]{0:T(128)}, f32[128]{0:T(128)S(1)}, u32[]{:S(2)}) copy-start(f32[128]{0:T(128)S(1)} %add_rsqrt_fusion.1) | copy-start | bytes 1540
  103.6 1.8 copy-start.6
  104.4 2.1 copy-start.39
  105.0 13.1 %copy-start.8 = (bf16[960,320]{0,1:T(8,128)(2,1)}, bf16[960,320]{0,1:T(8,128)(2,1)S(1)}, u32[]{:S(2)}) copy-start(bf16[960,320]{0,1:T(8,128)(2,1)S(1)} %reshape.329) | copy-start | bytes 1843204
  105.0 2.4 copy-start.12
  201.2 9.8 %copy-start.25 = (pred[128,1024]{0,1:T(8,128)(4,1)S(1)}, pred[128,1024]{0,1:T(8,128)(4,1)}, u32[]{:S(2)}) copy-start(pred[128,1024]{0,1:T(8,128)(4,1)} %fusion.28) | copy-start | bytes 393220
  201.4 11.0 %copy-start.20 = (bf16[128,15,64]{0,2,1:T(8,128)(2,1)}, bf16[128,15,64]{0,2,1:T(8,128)(2,1)S(1)}, u32[]{:S(2)}) copy-start(bf16[128,15,64]{0,2,1:T(8,128)(2,1)S(1)} %pad_maximum_fusion.9) | copy-start | bytes 737284
  211.0 1.4 copy-start.4
  211.1 3.0 copy-start.31
  212.4 3.1 copy-start
  215.5 2.0 copy-start.2
  217.5 10.8 %copy-start.18 = (bf16[5,64,3,128]{3,1,2,0:T(8,128)(2,1)}, bf16[5,64,3,128]{3,1,2,0:T(8,128)(2,1)S(1)}, u32[]{:S(2)}) copy-start(bf16[5,64,3,128]{3,1,2,0:T(8,128)(2,1)S(1)} %convolution_convert_fusion.10) | copy-start | bytes 737284
  217.5 1.0 copy-start.35
  217.5 10.8 %copy-start.11 = (bf16[1280,960]{1,0:T(8,128)(2,1)S(1)}, bf16[1280,960]{1,0:T(8,128)(2,1)}, u32[]{:S(2)}) copy-start(bf16[1280,960]{1,0:T(8,128)(2,1)} %reshape.345) | copy-start | bytes 7372804
  228.3 1.6 copy-start.29
  228.3 1.7 copy-start.24
  228.3 1.9 copy-start.27
  230.3 1.4 copy-start.45
  231.7 1.5 copy-start.43
  231.7 1.5 copy-start.44
  234.4 37.5 %all-to-all-start.1 = ((bf16[4,128,960]{1,2,0:T(8,128)(2,1)}), bf16[4,128,960]{1,2,0:T(8,128)(2,1)}, u32[]{:S(2)}, u32[]{:S(2)}) async-start(bf16[4,128,960]{1,2,0:T(8,128)(2,1)} %bitcast.236), calls=%async_computation.1 | async-start | bytes 1966080 | tf_op jit(solution)/shard_map/all_to_all | solution.py:105
  253.7 4.0 copy-start.28
  253.7 4.0 copy-start.46
  271.9 3.3 copy-start.3
  273.8 2.1 copy-start.19
  273.8 2.2 copy-start.26
  273.8 2.0 copy-start.40
  273.8 7.5 %slice-start = ((s8[7864320]{0:T(1024)(128)(4,1)}), s8[4194304]{0:T(1024)(128)(4,1)S(1)}, s32[]{:S(2)}) async-start(s8[7864320]{0:T(1024)(128)(4,1)} %bitcast.215), calls=%async_computation.13 | async-start | bytes 8388608
  275.2 0.7 copy-start.14
  276.0 5.4 %slice-start.1 = ((s8[7864320]{0:T(1024)(128)(4,1)}), s8[3670016]{0:T(1024)(128)(4,1)S(1)}, s32[]{:S(2)}) async-start(s8[7864320]{0:T(1024)(128)(4,1)} %bitcast.215), calls=%async_computation.14 | async-start | bytes 7340032
  276.0 5.4 %copy-start.32 = (bf16[1024,320]{0,1:T(8,128)(2,1)S(1)}, bf16[1024,320]{0,1:T(8,128)(2,1)}, u32[]{:S(2)}) copy-start(bf16[1024,320]{0,1:T(8,128)(2,1)} %copy-done.31) | copy-start | bytes 1966084
  281.4 2.8 copy-start.21
  284.2 1.9 copy-start.1
  287.7 37.5 %all-to-all-start.2 = ((bf16[8,128,640]{1,2,0:T(8,128)(2,1)}), bf16[8,128,640]{1,2,0:T(8,128)(2,1)}, u32[]{:S(2)}, u32[]{:S(2)}) async-start(bf16[8,128,640]{1,2,0:T(8,128)(2,1)} %pad_maximum_fusion.2), calls=%async_computation.2 | async-start | bytes 2621440 | tf_op jit(solution)/shard_map/all_to_all | solution.py:105
  292.0 68.8 %all-gather.11.cloned.1.call-start = ((), (), s32[]{:S(2)}) async-start(), calls=%async_computation.8 | async-start | bytes 3276800 | tf_op jit(solution)/shard_map/all_gather | solution.py:350
  325.1 2.4 copy-start.15
  325.1 2.4 copy-start.16
  326.7 0.7 copy-start.22
  328.4 135.6 %reduce-scatter.2.cloned.1.call-start = ((), (), s32[]{:S(2)}) async-start(), calls=%async_computation.9 | async-start | bytes 4423680 | tf_op jit(solution)/shard_map/reduce_scatter | solution.py:101
  334.4 13.0 %all-to-all-start.3 = ((bf16[4,128,240]{1,2,0:T(8,128)(2,1)}), bf16[4,128,240]{1,2,0:T(8,128)(2,1)}, u32[]{:S(2)}, u32[]{:S(2)}) async-start(bf16[4,128,240]{1,2,0:T(8,128)(2,1)} %bitcast.256), calls=%async_computation.3 | async-start | bytes 491520 | tf_op jit(solution)/shard_map/all_to_all | solution.py:115
  342.8 1.2 copy-start.9
  342.9 1.4 copy-start.23
  342.9 2.6 copy-start.7
  344.2 7.2 %copy-start.17 = (bf16[128,15,64]{0,2,1:T(8,128)(2,1)S(1)}, bf16[128,15,64]{0,2,1:T(8,128)(2,1)}, u32[]{:S(2)}) copy-start(bf16[128,15,64]{0,2,1:T(8,128)(2,1)} %maximum_convert_fusion) | copy-start | bytes 737284
  347.3 9.9 %all-to-all-start.4 = ((bf16[4,128,240]{1,2,0:T(8,128)(2,1)}), bf16[4,128,240]{1,2,0:T(8,128)(2,1)}, u32[]{:S(2)}, u32[]{:S(2)}) async-start(bf16[4,128,240]{1,2,0:T(8,128)(2,1)} %bitcast.255), calls=%async_computation.4 | async-start | bytes 491520 | tf_op jit(solution)/shard_map/all_to_all | solution.py:115
  357.3 23.9 %all-to-all-start = ((bf16[4,128,960]{1,2,0:T(8,128)(2,1)}), bf16[4,128,960]{1,2,0:T(8,128)(2,1)S(1)}, u32[]{:S(2)}, u32[]{:S(2)}) async-start(bf16[4,128,960]{1,2,0:T(8,128)(2,1)} %bitcast.235), calls=%async_computation | async-start | bytes 1966080 | tf_op jit(solution)/shard_map/all_to_all | solution.py:105
  365.5 0.9 copy-start.30
  381.1 84.3 %copy-start.42 = (f32[128]{0:T(128)S(1)}, f32[128]{0:T(128)}, u32[]{:S(2)}) copy-start(f32[128]{0:T(128)} %get-tuple-element.75) | copy-start | bytes 1540
  381.1 84.3 %copy-start.13 = (bf16[128,960]{0,1:T(8,128)(2,1)S(1)}, bf16[128,960]{0,1:T(8,128)(2,1)}, u32[]{:S(2)}) copy-start(bf16[128,960]{0,1:T(8,128)(2,1)} %param.23) | copy-start | bytes 737284
  381.1 84.3 %copy-start.38 = (f32[128]{0:T(128)S(1)}, f32[128]{0:T(128)}, u32[]{:S(2)}) copy-start(f32[128]{0:T(128)} %copy-done.37) | copy-start | bytes 1540
  381.1 84.3 %copy-start.41 = (f32[128]{0:T(128)S(1)}, f32[128]{0:T(128)}, u32[]{:S(2)}) copy-start(f32[128]{0:T(128)} %copy-done.40) | copy-start | bytes 1540
  381.2 0.9 copy-start.10
  382.1 85.5 %all-to-all-start.5 = ((bf16[8,128,640]{2,1,0:T(8,128)(2,1)}), bf16[8,128,640]{2,1,0:T(8,128)(2,1)S(1)}, u32[]{:S(2)}, u32[]{:S(2)}) async-start(bf16[8,128,640]{2,1,0:T(8,128)(2,1)} %pad_maximum_fusion.3), calls=%async_computation.5 | async-start | bytes 2621440 | tf_op jit(solution)/shard_map/all_to_all | solution.py:105
  385.7 101.4 %all-gather.13.cloned.1.call-start = ((), (), s32[]{:S(2)}) async-start(), calls=%async_computation.10 | async-start | bytes 2457600 | tf_op jit(solution)/shard_map/all_gather | solution.py:320
Sparse Core Ops, SparseCore 0:
  11.7 84.5 all-gather.14
  99.0 67.8 all-gather.16
  169.4 40.1 all-gather.8
  328.6 25.9 all-gather.10
  358.1 105.8 reduce-scatter.1
  465.4 21.6 all-gather.12
